TPU v7x, 32 devices: a whole 2x2x4 slice. The times are simulated.
32 devices in a mesh: lists: 4 (over y, x), points: 8 (over z, core).
Axes of the slice: x: 2, y: 2, z: 4, core: 2. Of those that a mesh axis runs over, the one named last changes fastest.
Arguments:
- child_centroids: float32 [1024, 768], P(('lists', 'points')), may hold values from -6 to 6
- child_sizes: int32 [1024], P(('lists', 'points')), may hold values from 1 to 256
- parent_of: int32 [1024], P(('lists', 'points')), may hold values from 0 to 511, as said below
- points: bfloat16 [49152, 768], P(('lists', 'points')), may hold values from -6 to 6
- assign: int32 [49152], P(('lists', 'points')), may hold values from 0 to 127
- codes: int32 [49152, 96], P(('lists', 'points')), may hold values from 0 to 255
- rotation: bfloat16 [768, 768], replicated, may hold values from -0.21875 to 0.21875
Outputs:
- merged_centroids: float32 [512, 768], P(('lists', 'points'))
- codeword_means: float32 [768, 256], replicated
Inputs may be any that keep to these rules, and one draw needn't show every extreme that they name: `parent_of`: every parent has exactly two children. Of the 32 children of one device, at most 16 have parents in one block of 128 consecutive parent numbers, and exactly 16 in some block.
All inputs are finite; a program needn't handle non-finite values.
Results may differ from a plain program's by a relative error of at most 0.0042.
Values may be sent and summed in bfloat16 or wider, within the bound.
No kernel may reach another device: no remote copies, remote signals or barrier semaphores. Data moves between devices by JAX's collectives and lax.ppermute only.
A program may use at most 64 MiB of HBM per device.

v0:
```python
import jax
import jax.numpy as jnp
from jax import lax
from jax.sharding import PartitionSpec as P

CODEWORDS = 256


def body(child_centroids, child_sizes, parent_of, points, assign, codes, rotation):
    columns = lax.axis_size("points")
    child_count = child_centroids.shape[0]
    feature_width = child_centroids.shape[1]
    owner_parents = columns * child_count // 2
    child_weight = child_sizes.astype(jnp.float32)
    weighted = child_weight[:, None] * child_centroids
    all_rows, all_mass, all_parent = (
        lax.all_gather(weighted, "lists", axis=0, tiled=True),
        lax.all_gather(child_weight, "lists", axis=0, tiled=True),
        lax.all_gather(parent_of.astype(jnp.float32), "lists", axis=0, tiled=True),
    )
    parent_whole = all_parent.astype(jnp.int32)
    first_parent = lax.axis_index("lists") * owner_parents
    owned_here = (parent_whole >= first_parent) & (parent_whole < first_parent + owner_parents)
    got_rows = jnp.where(owned_here[:, None], all_rows, 0.0)
    got_mass = jnp.where(owned_here, all_mass, 0.0)
    seg_target = jnp.where(owned_here, parent_whole - first_parent, 0)
    partial_sum = jax.ops.segment_sum(got_rows, seg_target, num_segments=owner_parents)
    partial_mass = jax.ops.segment_sum(got_mass, seg_target, num_segments=owner_parents)
    shard_rows = owner_parents // columns
    total_sum, total_mass = lax.psum((partial_sum, partial_mass), "points")
    merged_all = total_sum / total_mass[:, None]
    lowered = merged_all.astype(jnp.bfloat16)
    merged = lax.dynamic_slice_in_dim(
        merged_all, lax.axis_index("points") * shard_rows, shard_rows, 0
    )
    chosen = jnp.take(lowered, assign, axis=0)
    residual = (points.astype(jnp.float32) - chosen.astype(jnp.float32)).astype(jnp.bfloat16)
    rotated = jnp.dot(residual, rotation, preferred_element_type=jnp.float32).astype(jnp.bfloat16)
    point_count = points.shape[0]
    subspaces = codes.shape[1]
    sub_width = feature_width // subspaces
    block_rows = min(128, point_count)
    block_count = point_count // block_rows
    codeword_ids = jnp.arange(CODEWORDS, dtype=jnp.int32)

    def accumulate(carried, block_inputs):
        code_sums, code_counts = carried
        rot_blk, code_blk = block_inputs
        onehot = (code_blk[:, :, None] == codeword_ids[None, None, :]).astype(jnp.bfloat16)
        code_sums = code_sums + jnp.einsum(
            "pmd,pmk->mdk", rot_blk, onehot, preferred_element_type=jnp.float32
        )
        code_counts = code_counts + jnp.sum(onehot, axis=0, dtype=jnp.float32)
        return ((code_sums, code_counts), None)

    initial = (
        jnp.zeros((subspaces, sub_width, CODEWORDS), jnp.float32),
        jnp.zeros((subspaces, CODEWORDS), jnp.float32),
    )
    (code_sums, code_counts), _ = lax.scan(
        accumulate,
        initial,
        (
            rotated.reshape(block_count, block_rows, subspaces, sub_width),
            codes.reshape(block_count, block_rows, subspaces),
        ),
    )
    total_sums, total_counts = lax.psum(
        (code_sums.reshape(feature_width, CODEWORDS), code_counts), ("lists", "points")
    )
    means = total_sums.reshape(subspaces, sub_width, CODEWORDS) / (1.0 + total_counts[:, None, :])
    return (merged, means.reshape(feature_width, CODEWORDS))


def solution(mesh):
    in_specs = (
        P(("lists", "points"), None),
        P(("lists", "points")),
        P(("lists", "points")),
        P(("lists", "points"), None),
        P(("lists", "points")),
        P(("lists", "points"), None),
        P(),
    )
    out_specs = (P(("lists", "points"), None), P())
    return jax.shard_map(body, mesh=mesh, in_specs=in_specs, out_specs=out_specs, check_vma=False)
```

profile of v0, /device:TPU:0, one launch (start us, length us, event | category | flops | bytes accessed | tf_op | source)
XLA Modules:
  0.0 357.0 jit_solution(9061663071165604065)
XLA Ops:
  8.1 1.2 dynamic-slice
  11.5 11.3 %all-reduce.3 = (f32[128]{0:T(128)S(1)}, f32[128]{0:T(128)S(1)}) all-reduce(f32[128]{0:T(128)S(1)} %convert_dynamic-update-slice_fusion, f32[128]{0:T(128)S(1)} %convert_dynamic-update-slice_fusion.1), channel_id=1, replica_groups=mesh['lists'=4,'points'=8] {'lists'}, use_global_device_ids=true, to_apply=%add | all-reduce | flops 256 | bytes 2048
  23.8 9.0 %all_gather.10 = f32[128,768]{1,0:T(8,128)S(1)} all-gather(f32[32,768]{1,0:T(8,128)S(1)} %broadcast_multiply_fusion), channel_id=1, replica_groups=mesh['lists'=4,'points'=8] {'lists'}, dimensions={0}, use_global_device_ids=true | all-gather | bytes 491520 | tf_op jit(solution)/shard_map/all_gather | solution.py:17
  32.8 2.2 scatter_custom_fusion
  35.1 1.4 scatter_custom_fusion.1
  36.5 13.7 %psum.29 = f32[128]{0:T(128)S(1)} all-reduce(f32[128]{0:T(128)S(1)} %scatter_custom_fusion.1), channel_id=1, replica_groups=mesh['lists'=4,'points'=8] {'points'}, use_global_device_ids=true, to_apply=%region_3.4 | all-reduce | flops 128 | bytes 1024 | tf_op jit(solution)/shard_map/psum | solution.py:30
  51.0 1.0 reshape.30
  52.0 39.0 %all-reduce.7.cloned.1.call-done = f32[128,768]{1,0:T(8,128)} async-done(((f32[128,768]{1,0:T(8,128)}), f32[128,768]{1,0:T(8,128)}) %all-reduce.7.cloned.1.call-update) | async-done | bytes 393232 | tf_op jit(solution)/shard_map/psum | solution.py:30
  91.0 1.9 fusion.18
  92.9 5.7 %gather_fusion = bf16[1536,768]{1,0:T(8,128)(2,1)} fusion(bf16[128,768]{1,0:T(8,128)(2,1)S(1)} %get-tuple-element.81, s32[2048]{0:T(1024)S(1)} %pad_clamp_fusion), kind=kCustom, calls=%fused_computation | custom fusion | bytes 4724736 | tf_op jit(solution)/shard_map/jit(_take)/gather | solution.py:36
  98.6 6.0 %convolution_convert_fusion = bf16[1536,768]{1,0:T(8,128)(2,1)} fusion(bf16[768,768]{1,0:T(8,128)(2,1)S(1)} %copy-done, bf16[1536,768]{1,0:T(8,128)(2,1)} %param.12, bf16[1536,768]{1,0:T(8,128)(2,1)} %gather_fusion, pred[1536]{0:T(1024)(128)(4,1)S(1)} %compare_and_fusion), kind=kOutput, calls=%fused_computation.16 | convolution fusion | flops 1819017216 | bytes 8259072 | tf_op jit(solution)/shard_map/dot_general | solution.py:38
  104.6 2.8 copy.10
  107.4 3.1 reshape.29
  110.5 4.0 %copy.11 = bf16[12,128,96,8]{1,3,2,0:T(8,128)(2,1)} copy(bf16[12,128,96,8]{1,0,3,2:T(8,128)(2,1)} %reshape.29) | data formatting | bytes 4718592
  114.5 103.4 %while.13 = (s32[]{:T(128)}, f32[96,8,256]{2,1,0:T(8,128)S(1)}, f32[96,256]{1,0:T(8,128)S(1)}, bf16[12,128,96,8]{1,3,2,0:T(8,128)(2,1)}, s32[12,128,96]{1,0,2:T(8,128)}, /*index=5*/s32[]{:T(128)}, s32[]{:T(128)}) while((s32[]{:T(128)}, f32[96,8,256]{2,1,0:T(8,128)S(1)}, f32[96,256]{1,0:T(8,128)S(1)}, ...), condition=%wide.region_6.7_spmd.clone, body=%wide.region_4.6_spmd.clone.sunk | while | flops 66478080 | bytes 2359900 | solution.py:60
  115.6 5.1 %fusion.23 = f32[96,8,256]{2,1,0:T(8,128)S(1)} fusion(s32[128,96]{0,1:T(8,128)S(1)} %bitcast.19, f32[96,8,256]{2,1,0:T(8,128)S(1)} %get-tuple-element.124, pred[]{:T(512)S(6)} %compare.3, bf16[12,128,96,8]{1,3,2,0:T(8,128)(2,1)} %get-tuple-element.133, s32[]{:T(128)} %get-tuple-element.123), kind=kOutput, calls=%fused_computation.9.clone.1 | convolution fusion | flops 53870592 | bytes 1819137 | tf_op jit(solution)/shard_map/while/body/eval_jaxpr/pmd,pmk->mdk/dot_general | solution.py:50
  120.6 2.5 convert_reduce_fusion.2
  123.1 1.0 constant_dynamic-slice_fusion.3
  124.2 5.1 %fusion.23 = f32[96,8,256]{2,1,0:T(8,128)S(1)} fusion(s32[128,96]{0,1:T(8,128)S(1)} %bitcast.19, f32[96,8,256]{2,1,0:T(8,128)S(1)} %get-tuple-element.124, pred[]{:T(512)S(6)} %compare.3, bf16[12,128,96,8]{1,3,2,0:T(8,128)(2,1)} %get-tuple-element.133, s32[]{:T(128)} %get-tuple-element.123), kind=kOutput, calls=%fused_computation.9.clone.1 | convolution fusion | flops 53870592 | bytes 1819137 | tf_op jit(solution)/shard_map/while/body/eval_jaxpr/pmd,pmk->mdk/dot_general | solution.py:50
  129.2 2.5 convert_reduce_fusion.2
  131.7 1.0 constant_dynamic-slice_fusion.3
  132.8 5.1 %fusion.23 = f32[96,8,256]{2,1,0:T(8,128)S(1)} fusion(s32[128,96]{0,1:T(8,128)S(1)} %bitcast.19, f32[96,8,256]{2,1,0:T(8,128)S(1)} %get-tuple-element.124, pred[]{:T(512)S(6)} %compare.3, bf16[12,128,96,8]{1,3,2,0:T(8,128)(2,1)} %get-tuple-element.133, s32[]{:T(128)} %get-tuple-element.123), kind=kOutput, calls=%fused_computation.9.clone.1 | convolution fusion | flops 53870592 | bytes 1819137 | tf_op jit(solution)/shard_map/while/body/eval_jaxpr/pmd,pmk->mdk/dot_general | solution.py:50
  137.8 2.5 convert_reduce_fusion.2
  140.4 1.0 constant_dynamic-slice_fusion.3
  141.4 5.1 %fusion.23 = f32[96,8,256]{2,1,0:T(8,128)S(1)} fusion(s32[128,96]{0,1:T(8,128)S(1)} %bitcast.19, f32[96,8,256]{2,1,0:T(8,128)S(1)} %get-tuple-element.124, pred[]{:T(512)S(6)} %compare.3, bf16[12,128,96,8]{1,3,2,0:T(8,128)(2,1)} %get-tuple-element.133, s32[]{:T(128)} %get-tuple-element.123), kind=kOutput, calls=%fused_computation.9.clone.1 | convolution fusion | flops 53870592 | bytes 1819137 | tf_op jit(solution)/shard_map/while/body/eval_jaxpr/pmd,pmk->mdk/dot_general | solution.py:50
  146.5 2.5 convert_reduce_fusion.2
  149.0 1.0 constant_dynamic-slice_fusion.3
  150.0 5.1 %fusion.23 = f32[96,8,256]{2,1,0:T(8,128)S(1)} fusion(s32[128,96]{0,1:T(8,128)S(1)} %bitcast.19, f32[96,8,256]{2,1,0:T(8,128)S(1)} %get-tuple-element.124, pred[]{:T(512)S(6)} %compare.3, bf16[12,128,96,8]{1,3,2,0:T(8,128)(2,1)} %get-tuple-element.133, s32[]{:T(128)} %get-tuple-element.123), kind=kOutput, calls=%fused_computation.9.clone.1 | convolution fusion | flops 53870592 | bytes 1819137 | tf_op jit(solution)/shard_map/while/body/eval_jaxpr/pmd,pmk->mdk/dot_general | solution.py:50
  155.1 2.5 convert_reduce_fusion.2
  157.6 1.0 constant_dynamic-slice_fusion.3
  158.6 5.1 %fusion.23 = f32[96,8,256]{2,1,0:T(8,128)S(1)} fusion(s32[128,96]{0,1:T(8,128)S(1)} %bitcast.19, f32[96,8,256]{2,1,0:T(8,128)S(1)} %get-tuple-element.124, pred[]{:T(512)S(6)} %compare.3, bf16[12,128,96,8]{1,3,2,0:T(8,128)(2,1)} %get-tuple-element.133, s32[]{:T(128)} %get-tuple-element.123), kind=kOutput, calls=%fused_computation.9.clone.1 | convolution fusion | flops 53870592 | bytes 1819137 | tf_op jit(solution)/shard_map/while/body/eval_jaxpr/pmd,pmk->mdk/dot_general | solution.py:50
  163.7 2.5 convert_reduce_fusion.2
  166.2 1.0 constant_dynamic-slice_fusion.3
  167.3 5.1 %fusion.23 = f32[96,8,256]{2,1,0:T(8,128)S(1)} fusion(s32[128,96]{0,1:T(8,128)S(1)} %bitcast.19, f32[96,8,256]{2,1,0:T(8,128)S(1)} %get-tuple-element.124, pred[]{:T(512)S(6)} %compare.3, bf16[12,128,96,8]{1,3,2,0:T(8,128)(2,1)} %get-tuple-element.133, s32[]{:T(128)} %get-tuple-element.123), kind=kOutput, calls=%fused_computation.9.clone.1 | convolution fusion | flops 53870592 | bytes 1819137 | tf_op jit(solution)/shard_map/while/body/eval_jaxpr/pmd,pmk->mdk/dot_general | solution.py:50
  172.3 2.5 convert_reduce_fusion.2
  175.9 5.1 %fusion.23 = f32[96,8,256]{2,1,0:T(8,128)S(1)} fusion(s32[128,96]{0,1:T(8,128)S(1)} %bitcast.19, f32[96,8,256]{2,1,0:T(8,128)S(1)} %get-tuple-element.124, pred[]{:T(512)S(6)} %compare.3, bf16[12,128,96,8]{1,3,2,0:T(8,128)(2,1)} %get-tuple-element.133, s32[]{:T(128)} %get-tuple-element.123), kind=kOutput, calls=%fused_computation.9.clone.1 | convolution fusion | flops 53870592 | bytes 1819137 | tf_op jit(solution)/shard_map/while/body/eval_jaxpr/pmd,pmk->mdk/dot_general | solution.py:50
  180.9 2.5 convert_reduce_fusion.2
  184.5 5.1 %fusion.23 = f32[96,8,256]{2,1,0:T(8,128)S(1)} fusion(s32[128,96]{0,1:T(8,128)S(1)} %bitcast.19, f32[96,8,256]{2,1,0:T(8,128)S(1)} %get-tuple-element.124, pred[]{:T(512)S(6)} %compare.3, bf16[12,128,96,8]{1,3,2,0:T(8,128)(2,1)} %get-tuple-element.133, s32[]{:T(128)} %get-tuple-element.123), kind=kOutput, calls=%fused_computation.9.clone.1 | convolution fusion | flops 53870592 | bytes 1819137 | tf_op jit(solution)/shard_map/while/body/eval_jaxpr/pmd,pmk->mdk/dot_general | solution.py:50
  189.5 2.5 convert_reduce_fusion.2
  193.1 5.1 %fusion.23 = f32[96,8,256]{2,1,0:T(8,128)S(1)} fusion(s32[128,96]{0,1:T(8,128)S(1)} %bitcast.19, f32[96,8,256]{2,1,0:T(8,128)S(1)} %get-tuple-element.124, pred[]{:T(512)S(6)} %compare.3, bf16[12,128,96,8]{1,3,2,0:T(8,128)(2,1)} %get-tuple-element.133, s32[]{:T(128)} %get-tuple-element.123), kind=kOutput, calls=%fused_computation.9.clone.1 | convolution fusion | flops 53870592 | bytes 1819137 | tf_op jit(solution)/shard_map/while/body/eval_jaxpr/pmd,pmk->mdk/dot_general | solution.py:50
  198.2 2.5 convert_reduce_fusion.2
  201.7 5.1 %fusion.23 = f32[96,8,256]{2,1,0:T(8,128)S(1)} fusion(s32[128,96]{0,1:T(8,128)S(1)} %bitcast.19, f32[96,8,256]{2,1,0:T(8,128)S(1)} %get-tuple-element.124, pred[]{:T(512)S(6)} %compare.3, bf16[12,128,96,8]{1,3,2,0:T(8,128)(2,1)} %get-tuple-element.133, s32[]{:T(128)} %get-tuple-element.123), kind=kOutput, calls=%fused_computation.9.clone.1 | convolution fusion | flops 53870592 | bytes 1819137 | tf_op jit(solution)/shard_map/while/body/eval_jaxpr/pmd,pmk->mdk/dot_general | solution.py:50
  206.8 2.5 convert_reduce_fusion.2
  210.3 5.1 %fusion.23 = f32[96,8,256]{2,1,0:T(8,128)S(1)} fusion(s32[128,96]{0,1:T(8,128)S(1)} %bitcast.19, f32[96,8,256]{2,1,0:T(8,128)S(1)} %get-tuple-element.124, pred[]{:T(512)S(6)} %compare.3, bf16[12,128,96,8]{1,3,2,0:T(8,128)(2,1)} %get-tuple-element.133, s32[]{:T(128)} %get-tuple-element.123), kind=kOutput, calls=%fused_computation.9.clone.1 | convolution fusion | flops 53870592 | bytes 1819137 | tf_op jit(solution)/shard_map/while/body/eval_jaxpr/pmd,pmk->mdk/dot_general | solution.py:50
  215.4 2.5 convert_reduce_fusion.2
  218.9 1.4 constant_dynamic-slice_fusion.1
  220.3 126.8 %all-reduce.9.cloned.1.call-done = (f32[768,256]{1,0:T(8,128)}, f32[96,256]{1,0:T(8,128)}) async-done(((f32[768,256]{1,0:T(8,128)}, f32[96,256]{1,0:T(8,128)}), (f32[768,256]{1,0:T(8,128)}, f32[96,256]{1,0:T(8,128)})) %all-reduce.9.cloned.1.call-update) | async-done | bytes 884752 | tf_op jit(solution)/shard_map/psum | solution.py:68
  348.0 2.1 bitcast_divide_fusion
  (50 shorter events, 12.5 us)
Async XLA Ops:
  7.2 91.4 %copy-start = (bf16[768,768]{1,0:T(8,128)(2,1)S(1)}, bf16[768,768]{1,0:T(8,128)(2,1)}, u32[]{:S(2)}) copy-start(bf16[768,768]{1,0:T(8,128)(2,1)} %param.15) | copy-start | bytes 3538948
  7.2 44.8 %copy-start.6 = (s32[1536]{0:T(1024)S(1)}, s32[1536]{0:T(1024)}, u32[]{:S(2)}) copy-start(s32[1536]{0:T(1024)} %param.13) | copy-start | bytes 18436
  7.2 43.8 %copy-start.5 = (s32[1536,96]{0,1:T(8,128)S(1)}, s32[1536,96]{0,1:T(8,128)}, u32[]{:S(2)}) copy-start(s32[1536,96]{0,1:T(8,128)} %param.14) | copy-start | bytes 1769476
  7.2 83.8 %all-reduce.7.cloned.1.call-start = ((), (), s32[]{:S(2)}) async-start(), calls=%async_computation | async-start | bytes 786432 | tf_op jit(solution)/shard_map/psum | solution.py:30
  35.0 312.1 %all-reduce.9.cloned.1.call-start = ((), (), s32[]{:S(2)}) async-start(), calls=%async_computation.1 | async-start | bytes 1769472 | tf_op jit(solution)/shard_map/psum | solution.py:68
  110.5 4.0 %copy-start.1 = (f32[96,256]{1,0:T(8,128)S(1)}, f32[96,256]{1,0:T(8,128)}, u32[]{:S(2)}) copy-start(f32[96,256]{1,0:T(8,128)} %custom-call.1) | copy-start | bytes 294916
  110.5 4.0 %copy-start.3 = (f32[96,8,256]{2,1,0:T(8,128)S(1)}, f32[96,8,256]{2,1,0:T(8,128)}, u32[]{:S(2)}) copy-start(f32[96,8,256]{2,1,0:T(8,128)} %custom-call) | copy-start | bytes 2359300
  217.9 0.6 copy-start.2
  217.9 0.9 copy-start.4
Sparse Core Ops, SparseCore 0:
  35.1 55.8 all-reduce.6
  219.0 128.0 all-reduce.8
where the time goes:
time: 362 us; the launch traced here: 357 us
  waiting for transfers between devices  166 us (46%)
  matrix products  66.6 us (18%)
  other arithmetic  42.5 us (12%)
  blocking collectives  34.1 us (9%)
  local copies, waits for them, and re-layouts  32.6 us (9%)
  between operations  14.8 us (4%)
    psum x1, waiting for transfers between devices, body(): lax.psum((code_sums.reshape(feature_width, CODEWORDS), code_counts), ('li...  127 us
    dot_general x12, matrix products, accumulate(): jnp.einsum('pmd,pmk->mdk', rot_blk, onehot, preferred_element_type=jnp.fl...  60.6 us
    psum x1, waiting for transfers between devices, body(): total_sum, total_mass = lax.psum((partial_sum, partial_mass), 'points')  39 us
    reduce_sum x12, other arithmetic, accumulate(): code_counts = code_counts + jnp.sum(onehot, axis=0, dtype=jnp.float32)  29.6 us
    psum x1, blocking collectives, body(): total_sum, total_mass = lax.psum((partial_sum, partial_mass), 'points')  13.7 us
    dynamic_slice x12, local copies, waits for them, and re-layouts, body(): lax.scan(accumulate, initial, (rotated.reshape(block_count, block_rows, s...  12.4 us
    unnamed x1, blocking collectives  11.3 us
    all_gather x1, blocking collectives, body(): lax.all_gather(weighted, 'lists', axis=0, tiled=True)  9.01 us
  transfers between devices with their start and end apart: 2, of which 2 were waited for; matrix products, arithmetic and copies ran while one was open for 1% of the time, Pallas kernels for 0%

commit v1 on v0

v1 whole, which is shorter than its diff:
```python
import math

import jax
import jax.numpy as jnp
from jax import lax
from jax.experimental import pallas as pl
from jax.experimental.pallas import tpu as pltpu
from jax.sharding import PartitionSpec as P

CODEWORDS = 256
LOW = 32
HIGH = CODEWORDS // LOW
GROUP = 3
UNROLL = 8
LANES = 128
SWAP = ((0, 1), (1, 0))


def dot_nt(a, b):
    return lax.dot_general(a, b, (((1,), (1,)), ((), ())), preferred_element_type=jnp.float32)


def code_kernel(points_ref, assign_ref, codes_ref, rotation_ref, lowered_ref, out_ref, rot_ref, rest_ref, turned_ref):
    width, count = rot_ref.shape
    parents = lowered_ref.shape[0]
    sub_width = width // codes_ref.shape[0]
    groups = out_ref.shape[0]
    turned_ref[...] = rotation_ref[...].T
    piece = count // 3

    @pl.loop(0, 3)
    def _(step):
        span = pl.ds(pl.multiple_of(step * piece, piece), piece)
        parent_ids = lax.broadcasted_iota(jnp.int32, (parents, piece), 0)
        pick = jnp.where(parent_ids == assign_ref[:, span], 1.0, 0.0).astype(jnp.bfloat16)
        chosen = lax.dot_general(
            pick, lowered_ref[...], (((0,), (0,)), ((), ())), preferred_element_type=jnp.float32
        )
        rest_ref[span, :] = (points_ref[span, :].astype(jnp.float32) - chosen).astype(jnp.bfloat16)

    rows = width // 2

    @pl.loop(0, 2)
    def _(block):
        span = pl.ds(pl.multiple_of(block * rows, rows), rows)
        turned = turned_ref[span, :]
        for step in range(3):
            part = slice(step * piece, (step + 1) * piece)
            rotated = dot_nt(turned, rest_ref[part, :])
            rot_ref[span, part] = rotated.astype(jnp.bfloat16).astype(jnp.float32)

    def small(ids):
        return ids.astype(jnp.float32).astype(jnp.bfloat16)

    low_ids = small(lax.broadcasted_iota(jnp.int32, (LOW, count), 0))
    pair_ids = small(lax.broadcasted_iota(jnp.int32, (2 * sub_width, count), 0) // sub_width)
    high_ids = lax.broadcasted_iota(jnp.int32, (HIGH, count), 0)
    quarter = lax.broadcasted_iota(jnp.int32, (8, LANES), 1) // LOW
    line = lax.broadcasted_iota(jnp.int32, (8, LANES), 0)
    wide_line = lax.broadcasted_iota(jnp.int32, (8, CODEWORDS), 0)
    one, zero = jnp.ones((), jnp.bfloat16), jnp.zeros((), jnp.bfloat16)

    def moved(block, sub, place):
        turn = ((place - sub) * LOW) % LANES
        return pltpu.roll(block, turn, 1) if turn else block

    def one_group(group):
        weights, masked, tallies = [], [], []
        for sub in range(GROUP):
            index = group * GROUP + sub
            code = codes_ref[pl.ds(index, 1), :]
            low = small(jnp.broadcast_to(code & (LOW - 1), (LOW, count)))
            weights.append(jnp.where(low_ids == low, one, zero))
            high = code >> 5
            value = rot_ref[pl.ds(pl.multiple_of(index * sub_width, sub_width), sub_width), :]
            value = jnp.concatenate([value, value], axis=0).astype(jnp.bfloat16)
            behind = small(jnp.broadcast_to(high, (2 * sub_width, count))) - pair_ids
            for k in range(0, HIGH, 2):
                masked.append(jnp.where(behind == jnp.asarray(k, jnp.bfloat16), value, zero))
            tallies.append(jnp.where(high_ids == jnp.broadcast_to(high, (HIGH, count)), 1.0, 0.0))
        tallies.append(jnp.zeros((8, count), jnp.float32))
        weights.append(jnp.zeros((LANES - GROUP * LOW, count), jnp.bfloat16))
        result = dot_nt(
            jnp.concatenate(masked + [jnp.concatenate(tallies, axis=0).astype(jnp.bfloat16)], axis=0),
            jnp.concatenate(weights, axis=0),
        )
        lines = []
        for sub in range(GROUP):
            halves = []
            for half in range(2):
                total = None
                for place in range(4):
                    start = (sub * HIGH + half * 4 + place) * sub_width
                    part = jnp.where(quarter == place, moved(result[start : start + sub_width], sub, place), 0.0)
                    total = part if total is None else total + part
                halves.append(total)
            lines.append(jnp.concatenate(halves, axis=1))
        counts = jnp.zeros((8, CODEWORDS), jnp.float32)
        for sub in range(GROUP):
            start = GROUP * HIGH * sub_width + sub * HIGH
            block = result[start : start + HIGH]
            halves = []
            for half in range(2):
                total = None
                for place in range(4):
                    keep = (quarter == place) & (line == half * 4 + place)
                    part = jnp.where(keep, moved(block, sub, place), 0.0)
                    total = part if total is None else total + part
                halves.append(jnp.sum(total, axis=0, keepdims=True))
            row = jnp.broadcast_to(jnp.concatenate(halves, axis=1), (8, CODEWORDS))
            counts = jnp.where(wide_line == sub, row, counts)
        out_ref[group] = jnp.concatenate(lines + [counts], axis=0)

    @pl.loop(0, groups // UNROLL)
    def _(step):
        for k in range(UNROLL):
            one_group(step * UNROLL + k)


def code_sums(points, assign, codes, rotation, lowered):
    count, width = points.shape
    groups = codes.shape[0] // GROUP
    rows = GROUP * (width // codes.shape[0]) + 8
    return pl.pallas_call(
        code_kernel,
        out_shape=jax.ShapeDtypeStruct((groups, rows, CODEWORDS), jnp.float32),
        in_specs=[pl.BlockSpec(memory_space=pltpu.VMEM)] * 5,
        out_specs=pl.BlockSpec(memory_space=pltpu.VMEM),
        scratch_shapes=[
            pltpu.VMEM((width, count), jnp.float32),
            pltpu.VMEM((count, width), jnp.bfloat16),
            pltpu.VMEM((width, width), jnp.bfloat16),
        ],
        compiler_params=pltpu.CompilerParams(vmem_limit_bytes=48 << 20),
    )(points, assign, codes, rotation, lowered)


def body(child_centroids, child_sizes, parent_of, points, assign, codes, rotation):
    lists, rings = lax.axis_size("lists"), lax.axis_size("z")
    chips = lists * rings
    core = lax.axis_index("core")
    child_count, width = child_centroids.shape
    owner_parents = rings * child_count
    shard_rows = child_count // 2
    most = child_count // math.isqrt(lists)

    size = child_sizes[:, None]
    parent = parent_of[:, None]
    digits = jnp.concatenate([size >> 4, size & 15, parent >> 8, parent & 255], axis=1).astype(jnp.float32)
    sent = jnp.concatenate(
        [size.astype(jnp.float32) * child_centroids, jnp.pad(digits, ((0, 0), (0, LANES - 4)))], axis=1
    ).astype(jnp.bfloat16)
    owner = parent_of // owner_parents
    ids = jnp.arange(child_count, dtype=jnp.int32)
    earlier = (owner[:, None] == owner[None, :]) & (ids[None, :] < ids[:, None])
    slot = owner * most + jnp.sum(earlier, axis=1, dtype=jnp.int32)
    slots = jnp.arange(lists * most, dtype=jnp.int32)
    pack = (slots[:, None] == slot[None, :]).astype(jnp.bfloat16)
    packed = jnp.dot(pack, sent, preferred_element_type=jnp.float32).astype(jnp.bfloat16)
    packed = packed.reshape(lists, 1, most, width + LANES)
    packed = jnp.broadcast_to(packed, (lists, rings, most, width + LANES)).reshape(chips, most, width + LANES)
    near = lax.all_to_all(packed, ("lists", "z"), 0, 0).reshape(chips * most, width + LANES)
    near_parent = (near[:, width + 2].astype(jnp.int32) << 8) + near[:, width + 3].astype(jnp.int32)
    wanted = lax.axis_index("lists") * owner_parents + jnp.arange(owner_parents, dtype=jnp.int32)
    pick = (wanted[:, None] == near_parent[None, :]).astype(jnp.bfloat16)
    partial = jnp.dot(pick, near, preferred_element_type=jnp.float32)
    whole = partial + lax.ppermute(partial.astype(jnp.bfloat16), "core", SWAP).astype(jnp.float32)
    mass = whole[:, width] * 16.0 + whole[:, width + 1]
    merged_all = whole[:, :width] / mass[:, None]
    lowered = merged_all.astype(jnp.bfloat16)
    shard = lax.axis_index("z") * 2 + core
    merged = lax.dynamic_slice_in_dim(merged_all, shard * shard_rows, shard_rows, 0)

    sums = code_sums(points, assign[None, :], codes.T, rotation, lowered)
    groups, rows, _ = sums.shape
    half_groups = groups // 2
    splits = chips // half_groups
    sums = sums.reshape(2, half_groups, rows, splits, CODEWORDS // splits)
    sums = sums.transpose(0, 1, 3, 2, 4).reshape(2, chips, rows, CODEWORDS // splits)
    kept = lax.dynamic_index_in_dim(sums, core, 0, keepdims=False)
    given = lax.dynamic_index_in_dim(sums, 1 - core, 0, keepdims=False)
    taken = lax.ppermute(given, "core", SWAP)
    chip = (kept.astype(jnp.float32) + taken.astype(jnp.float32)).astype(jnp.bfloat16)
    total = jnp.sum(lax.all_to_all(chip, ("lists", "z"), 0, 0).astype(jnp.float32), axis=0)
    sub_width = (rows - 8) // GROUP
    tops = total[: rows - 8].reshape(GROUP, sub_width, -1)
    means = tops / (1.0 + total[rows - 8 : rows - 8 + GROUP, None, :])
    means = means.reshape(1, rows - 8, -1).astype(jnp.bfloat16)
    means = jnp.broadcast_to(means, (chips,) + means.shape[1:])
    mine = lax.all_to_all(means, ("lists", "z"), 0, 0)
    mine = mine.reshape(half_groups, splits, rows - 8, -1).transpose(0, 2, 1, 3).reshape(-1, CODEWORDS)
    other = lax.ppermute(mine, "core", SWAP)
    first = core == 0
    whole = jnp.concatenate([jnp.where(first, mine, other), jnp.where(first, other, mine)], axis=0)
    return merged, whole.astype(jnp.float32)


def solution(mesh):
    lists, points = mesh.devices.shape
    split = jax.sharding.Mesh(mesh.devices.reshape(lists, points // 2, 2), ("lists", "z", "core"))
    every = ("lists", "z", "core")
    in_specs = (P(every, None), P(every), P(every), P(every, None), P(every), P(every, None), P())
    out_specs = (P(every, None), P())
    return jax.shard_map(body, mesh=split, in_specs=in_specs, out_specs=out_specs, check_vma=False)
```

time: 362 us -> 74.3 us (0.21); the launches traced: 357 us -> 73.7 us
  waiting for transfers between devices: 166 us -> 18.2 us
  matrix products: 66.6 us -> 1.12 us
  other arithmetic: 42.5 us -> 4.31 us
  local copies, waits for them, and re-layouts: 32.6 us -> 4.74 us
  between operations: 14.8 us -> 0.75 us
  Pallas kernels: 0 us -> 10.5 us
  blocking collectives: 34.1 us -> 25.4 us
  starting transfers between devices: 0.08 us -> 8.65 us
    psum x2 -> x0, waiting for transfers between devices: 166 us -> none  [the longest x1 127 us: body(): lax.psum((code_sums.reshape(feature_width, CODEWORDS), code_counts), ('li...]
    dot_general x13 -> x2, matrix products: 66.6 us -> 1.12 us  [the longest x1 0.96 us: body(): partial = jnp.dot(pick, near, preferred_element_type=jnp.float32)]
    reduce_sum x12 -> x2, other arithmetic: 29.6 us -> 0.22 us  [the longest x1 0.18 us: body(): slot = owner * most + jnp.sum(earlier, axis=1, dtype=jnp.int32)]
    all_to_all x0 -> x2, blocking collectives: none -> 25.4 us  [the longest x1 13.8 us: body(): lax.all_to_all(chip, ('lists', 'z'), 0, 0).astype(jnp.float32)]
    all_to_all x0 -> x1, waiting for transfers between devices: none -> 14.8 us  [body(): lax.all_to_all(packed, ('lists', 'z'), 0, 0)]
    psum x1 -> x0, blocking collectives: 13.7 us -> none  [body(): total_sum, total_mass = lax.psum((partial_sum, partial_mass), 'points')]
    dynamic_slice x13 -> x1, local copies, waits for them, and re-layouts: 13.9 us -> 1.42 us  [body(): lax.dynamic_slice_in_dim(merged_all, shard * shard_rows, shard_rows, 0)]
    unnamed x1 -> x0, blocking collectives: 11.3 us -> none
  transfers between devices with their start and end apart: 2 -> 4, of which waited for: 2 -> 3; matrix products, arithmetic and copies ran while one was open for 1% -> 2% of each run, Pallas kernels for 0% -> 0%
where the time goes in v1:
time: 74.3 us; the launch traced here: 73.7 us
  blocking collectives  25.4 us (34%)
  waiting for transfers between devices  18.2 us (24%)
  Pallas kernels  10.5 us (14%)
  starting transfers between devices  8.65 us (12%)
  local copies, waits for them, and re-layouts  4.74 us (6%)
  other arithmetic  4.31 us (6%)
  matrix products  1.12 us (2%)
  between operations  0.75 us (1%)
    all_to_all x1, waiting for transfers between devices, body(): lax.all_to_all(packed, ('lists', 'z'), 0, 0)  14.8 us
    all_to_all x1, blocking collectives, body(): lax.all_to_all(chip, ('lists', 'z'), 0, 0).astype(jnp.float32)  13.8 us
    all_to_all x1, blocking collectives, body(): mine = lax.all_to_all(means, ('lists', 'z'), 0, 0)  11.6 us
    pallas_call x1, Pallas kernels, code_sums(): pl.pallas_call(code_kernel, out_shape=jax.ShapeDtypeStruct((groups, rows,...  10.5 us
    all_to_all x1, starting transfers between devices, body(): lax.all_to_all(packed, ('lists', 'z'), 0, 0)  8.44 us
    unnamed x9, local copies, waits for them, and re-layouts  2.45 us
    ppermute x1, waiting for transfers between devices, body(): taken = lax.ppermute(given, 'core', SWAP)  1.77 us
    ppermute x1, waiting for transfers between devices, body(): lax.ppermute(partial.astype(jnp.bfloat16), 'core', SWAP).astype(jnp.float32)  1.68 us
  transfers between devices with their start and end apart: 4, of which 3 were waited for; matrix products, arithmetic and copies ran while one was open for 2% of the time, Pallas kernels for 0%

profile of v1, /device:TPU:0, one launch (start us, length us, event | category | flops | bytes accessed | tf_op | source)
XLA Modules:
  0.0 73.7 jit_solution(2193910016611657609)
XLA Ops:
  0.6 0.0 copy-start.3
  0.6 0.7 %and_select_fusion = (s32[32]{0:T(128)S(1)}, s32[32,1]{0,1:T(1,128)S(1)}, s32[32,1]{0,1:T(1,128)S(1)}, s32[32,1]{0,1:T(1,128)S(1)}, s32[32,1]{0,1:T(1,128)S(1)}, /*index=5*/f32[32]{0:T(128)S(1)}) fusion(s32[32]{0:T(128)} %param.9, s32[32]{0:T(128)} %param.8), kind=kLoop, calls=%fused_computation.36 | loop fusion | flops 640 | bytes 1024 | tf_op jit(solution)/shard_map/jit(floor_divide)/jit(_where)/select_n | solution.py:153
  1.4 0.1 copy.14
  1.5 0.2 convert_reduce_fusion.1
  1.7 1.0 %multiply_convert_fusion = bf16[32,768]{1,0:T(8,128)(2,1)S(1)} fusion(f32[32,768]{1,0:T(8,128)} %param.7, f32[32]{0:T(128)S(1)} %get-tuple-element.16), kind=kLoop, calls=%fused_computation.15 | loop fusion | flops 49152 | bytes 147584 | tf_op jit(solution)/shard_map/convert
  2.7 0.2 convolution_convert_fusion
  2.8 0.8 %broadcast_in_dim.9 = bf16[4,4,16,896]{3,2,1,0:T(8,128)(2,1)} broadcast(bf16[4,16,896]{2,1,0:T(8,128)(2,1)S(1)} %bitcast.31), dimensions={0,2,3} | broadcast | bytes 573440 | tf_op jit(solution)/shard_map/broadcast_in_dim | solution.py:161
  3.6 0.0 copy-start
  3.6 8.4 %all-to-all-start = ((bf16[16,16,896]{2,1,0:T(8,128)(2,1)}), bf16[16,16,896]{2,1,0:T(8,128)(2,1)S(1)}, u32[]{:S(2)}, u32[]{:S(2)}) async-start(bf16[16,16,896]{2,1,0:T(8,128)(2,1)} %bitcast.5), calls=%async_computation | async-start | bytes 917504 | tf_op jit(solution)/shard_map/all_to_all | solution.py:162
  12.1 14.8 %all-to-all-done = bf16[16,16,896]{2,1,0:T(8,128)(2,1)S(1)} async-done(((bf16[16,16,896]{2,1,0:T(8,128)(2,1)}), bf16[16,16,896]{2,1,0:T(8,128)(2,1)S(1)}, u32[]{:S(2)}, u32[]{:S(2)}) %all-to-all-start) | async-done | bytes 458784 | tf_op jit(solution)/shard_map/all_to_all | solution.py:162
  26.9 0.2 add_reduce_fusion
  27.1 1.0 %fusion.22 = (bf16[128,896]{1,0:T(8,128)(2,1)}, f32[128,896]{1,0:T(8,128)S(1)}) fusion(bf16[256,896]{1,0:T(8,128)(2,1)S(1)} %bitcast.29, s32[256]{0:T(256)S(1)} %add_reduce_fusion, s32[128]{0:T(128)S(1)} %iota_add_fusion), kind=kOutput, calls=%fused_computation.52 | convolution fusion | flops 58867712 | bytes 1148416 | tf_op jit(solution)/shard_map/dot_general | solution.py:166
  28.0 0.0 collective-permute-start
  28.0 0.0 copy-done.3
  28.0 1.7 %collective-permute-done = bf16[128,896]{1,0:T(8,128)(2,1)S(1)} collective-permute-done((bf16[128,896]{1,0:T(8,128)(2,1)}, bf16[128,896]{1,0:T(8,128)(2,1)S(1)}, u32[]{:S(2)}, u32[]{:S(2)}) %collective-permute-start) | collective-permute-done | bytes 229408 | tf_op jit(solution)/shard_map/ppermute | solution.py:167
  29.8 0.2 fusion.4
  29.9 0.9 %fusion.20 = (bf16[128,768]{1,0:T(8,128)(2,1)S(1)}, f32[128,768]{1,0:T(8,128)}) fusion(f32[128]{0:T(128)S(1)} %fusion.4, f32[128,896]{1,0:T(8,128)S(1)} %convert_add_fusion), kind=kLoop, calls=%fused_computation.50 | loop fusion | flops 196608 | bytes 983552 | tf_op jit(solution)/shard_map/convert_element_type | solution.py:170
  30.8 0.0 copy-done
  30.8 0.0 copy-start.1
  30.8 1.3 %copy-done.1 = bf16[768,768]{1,0:T(8,128)(2,1)S(1)} copy-done((bf16[768,768]{1,0:T(8,128)(2,1)S(1)}, bf16[768,768]{1,0:T(8,128)(2,1)}, u32[]{:S(2)}) %copy-start.1) | copy-done | bytes 1179672
  32.1 0.0 copy-start.2
  32.1 1.1 %copy-done.2 = s32[1536,96]{0,1:T(8,128)S(1)} copy-done((s32[1536,96]{0,1:T(8,128)S(1)}, s32[1536,96]{0,1:T(8,128)}, u32[]{:S(2)}) %copy-start.2) | copy-done | bytes 589848
  33.2 10.5 %shard_map.86 = f32[32,32,256]{2,1,0:T(8,128)S(1)} custom-call(bf16[1536,768]{1,0:T(8,128)(2,1)S(1)} %copy-done, s32[1,1536]{1,0:T(1,128)S(1)} %broadcast_in_dim.10.assign_ref, s32[96,1536]{1,0:T(8,128)S(1)} %bitcast.27, bf16[768,768]{1,0:T(8,128)(2,1)S(1)} %copy-done.1, bf16[128,768]{1,0:T(8,128)(2,1)S(1)} %get-tuple-element.2.lowered_ref), custom_call_target="tpu_custom_call" | custom-call | tf_op jit(solution)/shard_map/pallas_call | solution.py:124
  43.8 0.2 collective-permute-start.1
  44.0 1.8 %collective-permute-done.1 = f32[16,32,256]{2,1,0:T(8,128)S(1)} collective-permute-done((f32[16,32,256]{2,1,0:T(8,128)S(1)}, f32[16,32,256]{2,1,0:T(8,128)S(1)}, u32[]{:S(2)}, u32[]{:S(2)}) %collective-permute-start.1) | collective-permute-done | bytes 524320 | tf_op jit(solution)/shard_map/ppermute | solution.py:182
  45.7 0.1 fusion
  45.8 13.8 %all_to_all.15 = bf16[16,32,256]{2,1,0:T(8,128)(2,1)S(1)} all-to-all(bf16[16,32,256]{2,1,0:T(8,128)(2,1)S(1)} %fusion), channel_id=1, replica_groups=mesh['lists'=4,'z'=4,'core'=2] {'lists','z'}, dimensions={0} | all-to-all | bytes 524288 | tf_op jit(solution)/shard_map/all_to_all | solution.py:184
  59.7 11.6 %all_to_all.16 = bf16[16,24,256]{2,1,0:T(8,128)(2,1)S(1)} all-to-all(bf16[16,24,256]{2,1,0:T(8,128)(2,1)S(1)} %broadcast_in_dim.11), channel_id=1, replica_groups=mesh['lists'=4,'z'=4,'core'=2] {'lists','z'}, dimensions={0} | all-to-all | bytes 393216 | tf_op jit(solution)/shard_map/all_to_all | solution.py:190
  71.3 0.0 collective-permute-start.2
  71.3 1.4 %constant_dynamic-slice_fusion = f32[16,768]{1,0:T(8,128)} fusion(f32[128,768]{1,0:T(8,128)} %get-tuple-element.3, s32[]{:T(128)S(6)} %select_n.28), kind=kLoop, calls=%fused_computation.40 | loop fusion | bytes 98308 | tf_op jit(solution)/shard_map/dynamic_slice | solution.py:172
  72.7 0.0 collective-permute-done.2
  72.8 0.9 %maximum_convert_fusion = f32[768,256]{1,0:T(8,128)} fusion(bf16[384,256]{1,0:T(8,128)(2,1)S(1)} %get-tuple-element.5, bf16[384,256]{1,0:T(8,128)(2,1)S(1)} %get-tuple-element.4), kind=kLoop, calls=%fused_computation.7 | loop fusion | flops 786432 | bytes 1179648 | tf_op jit(solution)/shard_map/convert_element_type | solution.py:195
  (11 shorter events, 0.2 us)
Async XLA Ops:
  0.6 27.4 %copy-start.3 = (s32[1536]{0:T(1024)S(1)}, s32[1536]{0:T(1024)}, u32[]{:S(2)}) copy-start(s32[1536]{0:T(1024)} %param.11) | copy-start | bytes 18436
  3.6 27.2 %copy-start = (bf16[1536,768]{1,0:T(8,128)(2,1)S(1)}, bf16[1536,768]{1,0:T(8,128)(2,1)}, u32[]{:S(2)}) copy-start(bf16[1536,768]{1,0:T(8,128)(2,1)} %points_ref.1) | copy-start | bytes 7077892
  3.6 23.2 %all-to-all-start = ((bf16[16,16,896]{2,1,0:T(8,128)(2,1)}), bf16[16,16,896]{2,1,0:T(8,128)(2,1)S(1)}, u32[]{:S(2)}, u32[]{:S(2)}) async-start(bf16[16,16,896]{2,1,0:T(8,128)(2,1)} %bitcast.5), calls=%async_computation | async-start | bytes 917504 | tf_op jit(solution)/shard_map/all_to_all | solution.py:162
  28.0 1.7 %collective-permute-start = (bf16[128,896]{1,0:T(8,128)(2,1)}, bf16[128,896]{1,0:T(8,128)(2,1)S(1)}, u32[]{:S(2)}, u32[]{:S(2)}) collective-permute-start(bf16[128,896]{1,0:T(8,128)(2,1)} %get-tuple-element.12), channel_id=1, source_target_pairs={{0,1},{1,0},{2,3},{3,2},{4,5},{5,4},{6,7},{7,6},{8,9},{9,8},{10,11... | collective-permute-start | bytes 688136 | tf_op jit(solution)/shard_map/ppermute | solution.py:167
  30.8 1.3 %copy-start.1 = (bf16[768,768]{1,0:T(8,128)(2,1)S(1)}, bf16[768,768]{1,0:T(8,128)(2,1)}, u32[]{:S(2)}) copy-start(bf16[768,768]{1,0:T(8,128)(2,1)} %rotation_ref.1) | copy-start | bytes 3538948
  32.1 1.1 %copy-start.2 = (s32[1536,96]{0,1:T(8,128)S(1)}, s32[1536,96]{0,1:T(8,128)}, u32[]{:S(2)}) copy-start(s32[1536,96]{0,1:T(8,128)} %param.12) | copy-start | bytes 1769476
  43.8 2.0 %collective-permute-start.1 = (f32[16,32,256]{2,1,0:T(8,128)S(1)}, f32[16,32,256]{2,1,0:T(8,128)S(1)}, u32[]{:S(2)}, u32[]{:S(2)}) collective-permute-start(f32[16,32,256]{2,1,0:T(8,128)S(1)} %dynamic-slice_bitcast_fusion), channel_id=1, source_target_pairs={{0,1},{1,0},{2,3},{3,2},{4,5},{5,4},{6,7},{7,6},{8,9},{9,8},{10,11... | collective-permute-start | bytes 1572872 | tf_op jit(solution)/shard_map/ppermute | solution.py:182
  71.3 1.4 %collective-permute-start.2 = (bf16[384,256]{1,0:T(8,128)(2,1)S(1)}, bf16[384,256]{1,0:T(8,128)(2,1)S(1)}, u32[]{:S(2)}, u32[]{:S(2)}) collective-permute-start(bf16[384,256]{1,0:T(8,128)(2,1)S(1)} %bitcast.30), channel_id=1, source_target_pairs={{0,1},{1,0},{2,3},{3,2},{4,5},{5,4},{6,7},{7,6},{8,9},{9,8},{10,11... | collective-permute-start | bytes 589832 | tf_op jit(solution)/shard_map/ppermute | solution.py:192

commit v2 on v1

v2 whole, which is shorter than its diff:
```python
import functools
import math

import jax
import jax.numpy as jnp
from jax import lax
from jax.experimental import pallas as pl
from jax.experimental.pallas import tpu as pltpu
from jax.sharding import PartitionSpec as P

CODEWORDS = 256
LOW = 32
HIGH = CODEWORDS // LOW
GROUP = 3
SIDE = 8
UNROLL = 3
FRACTION = 14.0
SIZE_BITS, PARENT_BITS, EXPONENT_BITS = 9, 13, 8
SLABS = 4
PIECES = 3
BLOCKS = 2
LANES = 128

FULL = 66_900_000
MOST = 66_200_000
SOME = 50_000_000
SWAP = ((0, 1), (1, 0))


def dot_nt(a, b):
    return lax.dot_general(a, b, (((1,), (1,)), ((), ())), preferred_element_type=jnp.float32)


def as_column(row):
    count = row.shape[1]
    shape = (count, count)
    here = lax.broadcasted_iota(jnp.int32, shape, 0) == lax.broadcasted_iota(jnp.int32, shape, 1)
    return jnp.sum(jnp.where(here, jnp.broadcast_to(row, shape), 0), axis=1, keepdims=True)


def power(exponent):
    return jnp.exp2(exponent)


def pack_kernel(owner_parents, child_hbm, size_hbm, parent_hbm, out_ref, child_ref, size_ref, parent_ref, sems):
    copies = [
        pltpu.make_async_copy(source, target, sems.at[k])
        for k, (source, target) in enumerate(
            ((child_hbm, child_ref), (size_hbm, size_ref), (parent_hbm, parent_ref))
        )
    ]
    for copy in copies:
        copy.start()
    for copy in copies:
        copy.wait()
    lists, rings, most, width = out_ref.shape
    count = child_ref.shape[0]
    parent_row = parent_ref[...]
    parent = as_column(parent_row)
    size = as_column(size_ref[...])
    owner_row, owner = parent_row // owner_parents, parent // owner_parents
    shape = (count, count)
    before = lax.broadcasted_iota(jnp.int32, shape, 0) < lax.broadcasted_iota(jnp.int32, shape, 1)
    earlier = jnp.where((owner == owner_row) & before, 1, 0)
    slot = owner_row * most + jnp.sum(earlier, axis=0, keepdims=True)
    slots = lax.broadcasted_iota(jnp.int32, (lists * most, count), 0)
    pack = jnp.where(slots == slot, 1.0, 0.0).astype(jnp.bfloat16)
    child = child_ref[...]
    top = jnp.max(jnp.abs(child), axis=1, keepdims=True)
    exponent = jnp.ceil(jnp.log2(jnp.maximum(top, 1e-30)))
    scaled = jnp.floor(child * power(FRACTION - exponent) + 0.5)
    word = size + (parent << SIZE_BITS)
    word = word + ((exponent.astype(jnp.int32) + 128) << (SIZE_BITS + PARENT_BITS))
    lane = lax.broadcasted_iota(jnp.int32, (count, LANES), 1)
    bit = (jnp.broadcast_to(word, (count, LANES)) >> jnp.minimum(lane, 31)) & 1
    marked = 2.0 * jnp.floor(scaled[:, :LANES] * 0.5) + bit.astype(jnp.float32)
    sent = jnp.concatenate([marked, scaled[:, LANES:]], axis=1)
    upper = jnp.floor(sent * (1.0 / 128.0))
    lower = sent - upper * 128.0
    packed = 128.0 * jnp.dot(pack, upper.astype(jnp.bfloat16), preferred_element_type=jnp.float32)
    packed = packed + jnp.dot(pack, lower.astype(jnp.bfloat16), preferred_element_type=jnp.float32)
    for k in range(lists):
        block = packed[k * most : (k + 1) * most].astype(jnp.int32).astype(jnp.int16)
        for ring in range(rings):
            out_ref[k, ring] = block


def merge_kernel(near_ref, after_ref, out_ref):
    del after_ref
    parents = out_ref.shape[0]
    first = lax.axis_index("lists") * parents
    width = out_ref.shape[1] - LANES
    near = near_ref[...].astype(jnp.int32)
    bits = (near[:, :LANES] & 1).astype(jnp.float32).astype(jnp.bfloat16)
    shape = (LANES, LANES)
    line, lane = lax.broadcasted_iota(jnp.int32, shape, 0), lax.broadcasted_iota(jnp.int32, shape, 1)
    values = jnp.zeros(shape, jnp.float32)
    start = 0
    for k, length in enumerate((SIZE_BITS, PARENT_BITS, EXPONENT_BITS)):
        keep = (lane == k) & (line >= start) & (line < start + length)
        value = (1 << jnp.minimum(jnp.maximum(line - start, 0), length)).astype(jnp.float32)
        values = jnp.where(keep, value, values)
        start += length
    note = jnp.dot(bits, values.astype(jnp.bfloat16), preferred_element_type=jnp.float32)
    size, parent, exponent = note[:, 0:1], note[:, 1:2], note[:, 2:3] - 128.0
    wanted = (lax.broadcasted_iota(jnp.int32, (near.shape[0], parents), 1) + first).astype(jnp.float32)
    pick = jnp.where(parent == wanted, 1.0, 0.0).astype(jnp.bfloat16)
    value = near.astype(jnp.float32) * (size * power(exponent - FRACTION))
    upper = value.astype(jnp.bfloat16)
    lower = (value - upper.astype(jnp.float32)).astype(jnp.bfloat16)

    def picked(rows):
        return lax.dot_general(pick, rows, (((0,), (0,)), ((), ())), preferred_element_type=jnp.float32)

    out_ref[:, :width] = picked(upper) + picked(lower)
    lane = lax.broadcasted_iota(jnp.int32, note.shape, 1)
    out_ref[:, width:] = picked(jnp.where(lane == 0, size, 0.0).astype(jnp.bfloat16))


def rotate_kernel(points_hbm, rotation_hbm, out_hbm, turned_hbm, points_ref, rotation_ref, out_ref, turned_ref, in_sems, out_sems):
    width, count = out_ref.shape
    piece, rows = count // PIECES, width // BLOCKS
    fetch = pltpu.make_async_copy(rotation_hbm, rotation_ref, in_sems.at[PIECES])
    fetch.start()
    parts = [slice(step * piece, (step + 1) * piece) for step in range(PIECES)]
    blocks = [slice(step * rows, (step + 1) * rows) for step in range(BLOCKS)]
    fetches = [
        pltpu.make_async_copy(points_hbm.at[part], points_ref.at[part], in_sems.at[k]) for k, part in enumerate(parts)
    ]
    for copy in fetches:
        copy.start()
    fetch.wait()
    turned_ref[...] = rotation_ref[...].T
    stores = [pltpu.make_async_copy(turned_ref, turned_hbm, out_sems.at[PIECES * BLOCKS])]
    stores[0].start()
    for k, part in enumerate(parts):
        fetches[k].wait()
        for j, block in enumerate(blocks):
            out_ref[block, part] = dot_nt(turned_ref[block, :], points_ref[part, :])
            store = pltpu.make_async_copy(
                out_ref.at[block, part], out_hbm.at[0, block, part], out_sems.at[k * BLOCKS + j]
            )
            store.start()
            stores.append(store)
    for store in stores:
        store.wait()


def code_kernel(
    whole_ref, turned_hbm, rotated_hbm, assign_ref, codes_ref,
    out_ref, merged_ref, all_ref, rot_ref, pick_ref, turned_ref, sems,
):
    width, count = rot_ref.shape
    parents = all_ref.shape[0]
    sub_width = width // codes_ref.shape[0]
    steps = codes_ref.shape[0] // (SIDE * UNROLL)
    rows = width // steps
    fetch = pltpu.make_async_copy(turned_hbm, turned_ref, sems.at[steps])
    fetch.start()

    def fetched(step):
        span = pl.ds(pl.multiple_of(step * rows, rows), rows)
        return pltpu.make_async_copy(rotated_hbm.at[0, span], rot_ref.at[span], sems.at[step])

    for step in range(steps):
        fetched(step).start()
    all_ref[...] = whole_ref[:, :width] / whole_ref[:, width : width + 1]
    shard_rows = merged_ref.shape[0]
    shard = lax.axis_index("z") * 2 + lax.axis_index("core")
    merged_ref[...] = all_ref[pl.ds(pl.multiple_of(shard * shard_rows, shard_rows), shard_rows), :]
    lowered = all_ref[...].astype(jnp.bfloat16)
    ids = lax.broadcasted_iota(jnp.int32, (parents, count), 0)
    pick = jnp.where(ids == assign_ref[...], 1.0, 0.0).astype(jnp.bfloat16)
    pick_ref[:parents, :] = pick
    pick_ref[parents:, :] = pick
    piece = count // PIECES

    def correct(step):
        span = pl.ds(pl.multiple_of(step * rows, rows), rows)
        parent = dot_nt(turned_ref[span, :], lowered)
        upper = parent.astype(jnp.bfloat16)
        lower = (parent - upper.astype(jnp.float32)).astype(jnp.bfloat16)
        both = jnp.concatenate([upper, lower], axis=1)
        fetched(step).wait()
        for k in range(PIECES):
            part = slice(k * piece, (k + 1) * piece)
            chosen = jnp.dot(both, pick_ref[:, part], preferred_element_type=jnp.float32)
            rot_ref[span, part] = rot_ref[span, part] - chosen

    def small(ids):
        return ids.astype(jnp.float32).astype(jnp.bfloat16)

    tile = 2 * sub_width
    low_ids = [small(lax.broadcasted_iota(jnp.int32, (tile, count), 0) + start) for start in range(0, LOW, tile)]
    pair_ids = small(lax.broadcasted_iota(jnp.int32, (tile, count), 0) // sub_width)
    high_ids = small(lax.broadcasted_iota(jnp.int32, (tile, count), 0) % HIGH)
    first_half = lax.broadcasted_iota(jnp.int32, (tile, count), 0) < HIGH
    spot = lax.broadcasted_iota(jnp.int32, (8, LANES), 1) // LOW
    line = lax.broadcasted_iota(jnp.int32, (8, LANES), 0)
    wide_line = lax.broadcasted_iota(jnp.int32, (8, CODEWORDS), 0)
    one, zero = jnp.ones((), jnp.bfloat16), jnp.zeros((), jnp.bfloat16)
    spots = LANES // LOW

    def part(rows, sub, place):
        rows = rows[:, sub // spots * LANES : (sub // spots + 1) * LANES]
        turn = (place - sub) % spots * LOW
        return pltpu.roll(rows, turn, 1) if turn else rows

    def spread(base):
        weights, masked, highs = [], [], []
        for sub in range(SIDE):
            index = base + sub
            code = codes_ref[pl.ds(index, 1), :]
            low = small(jnp.broadcast_to(code & (LOW - 1), (tile, count)))
            weights += [jnp.where(ids == low, one, zero) for ids in low_ids]
            value = rot_ref[pl.ds(pl.multiple_of(index * sub_width, sub_width), sub_width), :]
            value = jnp.concatenate([value, value], axis=0).astype(jnp.bfloat16)
            high = jnp.broadcast_to(code // LOW, (tile, count))
            highs.append(high)
            behind = small(high) - pair_ids
            for k in range(0, HIGH, 2):
                masked.append(jnp.where(behind == jnp.asarray(k, jnp.bfloat16), value, zero))
        for sub in range(0, SIDE, 2):
            high = small(jnp.where(first_half, highs[sub], highs[sub + 1]))
            masked.append(jnp.where(high_ids == high, one, zero))
        result = dot_nt(jnp.concatenate(masked, axis=0), jnp.concatenate(weights, axis=0))
        sums, counts = [], []
        for sub in range(SIDE):
            start = sub * HIGH * sub_width
            tally = result[SIDE * HIGH * sub_width + sub * HIGH :][:HIGH]
            halves, tallies = [], []
            for first in range(0, HIGH, spots):
                total, counted = None, None
                for k in range(first, first + spots):
                    piece = part(result[start + k * sub_width :][:sub_width], sub, k)
                    total = piece if total is None else jnp.where(spot == k % spots, piece, total)
                    piece = jnp.where(line == k, part(tally, sub, k), 0.0)
                    counted = piece if counted is None else jnp.where(spot == k % spots, piece, counted)
                halves.append(total)
                tallies.append(jnp.sum(counted, axis=0, keepdims=True))
            sums.append(halves)
            counts.append(tallies)
        return sums, counts

    fetch.wait()
    correct(0)
    for step in range(steps):
        if step + 1 < steps:
            correct(step + 1)
        sums, counts = [], []
        for k in range(UNROLL):
            more_sums, more_counts = spread((step * UNROLL + k) * SIDE)
            sums += more_sums
            counts += more_counts
        for k in range(SIDE * UNROLL // GROUP):
            mine = range(k * GROUP, (k + 1) * GROUP)
            lines = [jnp.concatenate(sums[sub], axis=1) for sub in mine]
            tally = jnp.zeros((8, CODEWORDS), jnp.float32)
            for place, sub in enumerate(mine):
                row = jnp.broadcast_to(jnp.concatenate(counts[sub], axis=1), (8, CODEWORDS))
                tally = jnp.where(wide_line == place, row, tally)
            out_ref[step * (SIDE * UNROLL // GROUP) + k] = jnp.concatenate(lines + [tally], axis=0)


def whole(count):
    return [pl.BlockSpec(memory_space=pltpu.VMEM)] * count


def anywhere(count):
    return [pl.BlockSpec(memory_space=pl.ANY)] * count


def shaped(shape, kind=jnp.float32):
    return jax.ShapeDtypeStruct(shape, kind)


def body(child_centroids, child_sizes, parent_of, points, assign, codes, rotation):
    lists, rings = lax.axis_size("lists"), lax.axis_size("z")
    chips = lists * rings
    core = lax.axis_index("core")
    child_count, width = child_centroids.shape
    count, subspaces = codes.shape
    owner_parents = rings * child_count
    shard_rows = child_count // 2
    most = child_count // math.isqrt(lists)
    wide = width + LANES

    packed = pl.pallas_call(
        functools.partial(pack_kernel, owner_parents),
        out_shape=shaped((lists, rings, most, width), jnp.int16),
        in_specs=anywhere(3),
        out_specs=whole(1)[0],
        scratch_shapes=[
            pltpu.VMEM((child_count, width), jnp.float32),
            pltpu.VMEM((1, child_count), jnp.int32),
            pltpu.VMEM((1, child_count), jnp.int32),
            pltpu.SemaphoreType.DMA((3,)),
        ],
        compiler_params=pltpu.CompilerParams(vmem_limit_bytes=FULL),
    )(child_centroids, child_sizes[None, :], parent_of[None, :])
    near = lax.all_to_all(packed.reshape(chips, most, width), ("lists", "z"), 0, 0)
    rotated, turned = pl.pallas_call(
        rotate_kernel,
        out_shape=(shaped((SLABS, width, count)), shaped((width, width), jnp.bfloat16)),
        in_specs=anywhere(2),
        out_specs=tuple(anywhere(2)),
        scratch_shapes=[
            pltpu.VMEM((count, width), jnp.bfloat16),
            pltpu.VMEM((width, width), jnp.bfloat16),
            pltpu.VMEM((width, count), jnp.float32),
            pltpu.VMEM((width, width), jnp.bfloat16),
            pltpu.SemaphoreType.DMA((PIECES + 1,)),
            pltpu.SemaphoreType.DMA((PIECES * BLOCKS + 1,)),
        ],
        compiler_params=pltpu.CompilerParams(vmem_limit_bytes=MOST),
        cost_estimate=pl.CostEstimate(flops=2 * width * width * count, bytes_accessed=10 << 20, transcendentals=0),
    )(points, rotation)
    mine = pl.pallas_call(
        merge_kernel,
        out_shape=shaped((owner_parents, wide)),
        in_specs=whole(1) + anywhere(1),
        out_specs=whole(1)[0],
        compiler_params=pltpu.CompilerParams(vmem_limit_bytes=SOME),
    )(near.reshape(chips * most, width), rotated)
    sums_of_list = mine + lax.ppermute(mine, "core", SWAP)
    groups = subspaces // GROUP
    rows = GROUP * (width // subspaces) + 8
    sums, merged = pl.pallas_call(
        code_kernel,
        out_shape=(shaped((groups, rows, CODEWORDS)), shaped((shard_rows, width))),
        in_specs=whole(1) + anywhere(2) + whole(2),
        out_specs=tuple(whole(2)),
        scratch_shapes=[
            pltpu.VMEM((owner_parents, width), jnp.float32),
            pltpu.VMEM((width, count), jnp.float32),
            pltpu.VMEM((2 * owner_parents, count), jnp.bfloat16),
            pltpu.VMEM((width, width), jnp.bfloat16),
            pltpu.SemaphoreType.DMA((subspaces // (SIDE * UNROLL) + 1,)),
        ],
        compiler_params=pltpu.CompilerParams(vmem_limit_bytes=SOME),
    )(sums_of_list, turned, rotated, assign[None, :], codes.T)

    half_groups = groups // 2
    splits = chips // half_groups
    sums = sums.reshape(2, half_groups, rows, splits, CODEWORDS // splits)
    sums = sums.transpose(0, 1, 3, 2, 4).reshape(2, chips, rows, CODEWORDS // splits)
    kept = lax.dynamic_index_in_dim(sums, core, 0, keepdims=False)
    given = lax.dynamic_index_in_dim(sums, 1 - core, 0, keepdims=False)
    taken = lax.ppermute(given, "core", SWAP)
    chip = (kept.astype(jnp.float32) + taken.astype(jnp.float32)).astype(jnp.bfloat16)
    total = jnp.sum(lax.all_to_all(chip, ("lists", "z"), 0, 0).astype(jnp.float32), axis=0)
    sub_width = (rows - 8) // GROUP
    tops = total[: rows - 8].reshape(GROUP, sub_width, -1)
    means = tops / (1.0 + total[rows - 8 : rows - 8 + GROUP, None, :])
    means = means.reshape(1, rows - 8, -1).astype(jnp.bfloat16)
    means = jnp.broadcast_to(means, (chips,) + means.shape[1:])
    mine = lax.all_to_all(means, ("lists", "z"), 0, 0)
    mine = mine.reshape(half_groups, splits, rows - 8, -1).transpose(0, 2, 1, 3).reshape(-1, CODEWORDS)
    other = lax.ppermute(mine, "core", SWAP)
    first = core == 0
    means = jnp.concatenate([jnp.where(first, mine, other), jnp.where(first, other, mine)], axis=0)
    return merged, means.astype(jnp.float32)


def solution(mesh):
    lists, points = mesh.devices.shape
    split = jax.sharding.Mesh(mesh.devices.reshape(lists, points // 2, 2), ("lists", "z", "core"))
    every = ("lists", "z", "core")
    in_specs = (P(every, None), P(every), P(every), P(every, None), P(every), P(every, None), P())
    out_specs = (P(every, None), P())
    return jax.shard_map(body, mesh=split, in_specs=in_specs, out_specs=out_specs, check_vma=False)
```

time: 74.3 us -> 69.1 us (0.930)
  Pallas kernels: 10.5 us -> 18.4 us
  waiting for transfers between devices: 18.2 us -> 13.3 us
  local copies, waits for them, and re-layouts: 4.74 us -> 1.14 us
  other arithmetic: 4.31 us -> 1.2 us
  matrix products: 1.12 us -> 0 us
    pallas_call x1 -> x4, Pallas kernels: 10.5 us -> 18.4 us  [the longest x1 10.7 us: body(): pl.pallas_call(code_kernel, out_shape=(shaped((groups, rows, CODEWORDS)),...]
    all_to_all x1, waiting for transfers between devices: 14.8 us -> 8.3 us  [body(): lax.all_to_all(packed.reshape(chips, most, width), ('lists', 'z'), 0, 0)]
    ppermute x1, waiting for transfers between devices: 0.02 us -> 1.44 us  [body(): other = lax.ppermute(mine, 'core', SWAP)]
    dynamic_slice x1 -> x0, local copies, waits for them, and re-layouts: 1.42 us -> none  [body(): lax.dynamic_slice_in_dim(merged_all, shard * shard_rows, shard_rows, 0)]
    unnamed x9 -> x6, local copies, waits for them, and re-layouts: 2.45 us -> 1.07 us
    dot_general x2 -> x0, matrix products: 1.12 us -> none  [the longest x1 0.96 us: body(): partial = jnp.dot(pick, near, preferred_element_type=jnp.float32)]
    another operation x2 -> x0, other arithmetic: 0.98 us -> none
    convert_element_type x2 -> x1, other arithmetic: 1.81 us -> 0.94 us  [body(): return (merged, means.astype(jnp.float32))]
  transfers between devices with their start and end apart: 4 -> 4, of which waited for: 3 -> 4; matrix products, arithmetic and copies ran while one was open for 2% -> 0% of each run, Pallas kernels for 0% -> 7%
where the time goes in v2:
time: 69.1 us; the launch traced here: 68.7 us
  blocking collectives  25.4 us (37%)
  Pallas kernels  18.4 us (27%)
  waiting for transfers between devices  13.3 us (19%)
  starting transfers between devices  8.61 us (12%)
  other arithmetic  1.2 us (2%)
  local copies, waits for them, and re-layouts  1.14 us (2%)
  between operations  0.76 us (1%)
    all_to_all x1, blocking collectives, body(): lax.all_to_all(chip, ('lists', 'z'), 0, 0).astype(jnp.float32)  13.8 us
    all_to_all x1, blocking collectives, body(): mine = lax.all_to_all(means, ('lists', 'z'), 0, 0)  11.6 us
    pallas_call x1, Pallas kernels, body(): pl.pallas_call(code_kernel, out_shape=(shaped((groups, rows, CODEWORDS)),...  10.7 us
    all_to_all x1, starting transfers between devices, body(): lax.all_to_all(packed.reshape(chips, most, width), ('lists', 'z'), 0, 0)  8.33 us
    all_to_all x1, waiting for transfers between devices, body(): lax.all_to_all(packed.reshape(chips, most, width), ('lists', 'z'), 0, 0)  8.3 us
    pallas_call x1, Pallas kernels, body(): pl.pallas_call(rotate_kernel, out_shape=(shaped((SLABS, width, count)), s...  5.08 us
    pallas_call x1, Pallas kernels, body(): pl.pallas_call(functools.partial(pack_kernel, owner_parents), out_shape=s...  1.98 us
    ppermute x1, waiting for transfers between devices, body(): sums_of_list = mine + lax.ppermute(mine, 'core', SWAP)  1.77 us
  transfers between devices with their start and end apart: 4, of which 4 were waited for; matrix products, arithmetic and copies ran while one was open for 0% of the time, Pallas kernels for 7%

profile of v2, /device:TPU:0, one launch (start us, length us, event | category | flops | bytes accessed | tf_op | source)
XLA Modules:
  0.0 68.7 jit_solution(11033996348277805300)
XLA Ops:
  0.6 2.0 %shard_map.86 = s16[4,4,16,768]{3,2,1,0:T(8,128)(2,1)} custom-call(f32[32,768]{1,0:T(8,128)} %child_hbm.1, s32[1,32]{1,0:T(1,128)} %bitcast.23, s32[1,32]{1,0:T(1,128)} %bitcast.24), custom_call_target="tpu_custom_call" | custom-call | tf_op jit(solution)/shard_map/pallas_call | solution.py:288
  2.6 8.3 %all-to-all-start = ((s16[16,16,768]{2,1,0:T(8,128)(2,1)}), s16[16,16,768]{2,1,0:T(8,128)(2,1)S(1)}, u32[]{:S(2)}, u32[]{:S(2)}) async-start(s16[16,16,768]{2,1,0:T(8,128)(2,1)} %bitcast.21), calls=%async_computation | async-start | bytes 786432 | tf_op jit(solution)/shard_map/all_to_all | solution.py:301
  11.0 5.1 %shard_map.87 = (f32[4,768,1536]{2,1,0:T(8,128)}, bf16[768,768]{1,0:T(8,128)(2,1)}) custom-call(bf16[1536,768]{1,0:T(8,128)(2,1)} %points_hbm.1, bf16[768,768]{1,0:T(8,128)(2,1)} %rotation_hbm.1), custom_call_target="tpu_custom_call" | custom-call | flops 1811939328 | bytes 10485760 | tf_op jit(solution)/shard_map/pallas_call | solution.py:302
  16.0 8.3 %all-to-all-done = s16[16,16,768]{2,1,0:T(8,128)(2,1)S(1)} async-done(((s16[16,16,768]{2,1,0:T(8,128)(2,1)}), s16[16,16,768]{2,1,0:T(8,128)(2,1)S(1)}, u32[]{:S(2)}, u32[]{:S(2)}) %all-to-all-start) | async-done | bytes 393248 | tf_op jit(solution)/shard_map/all_to_all | solution.py:301
  24.3 0.0 copy-start.2
  24.3 0.0 copy-start
  24.3 0.7 shard_map.88
  25.0 0.1 collective-permute-start
  25.1 0.0 copy-done.2
  25.1 1.8 %collective-permute-done = f32[128,896]{1,0:T(8,128)S(1)} collective-permute-done((f32[128,896]{1,0:T(8,128)S(1)}, f32[128,896]{1,0:T(8,128)S(1)}, u32[]{:S(2)}, u32[]{:S(2)}) %collective-permute-start) | collective-permute-done | bytes 458784 | tf_op jit(solution)/shard_map/ppermute | solution.py:325
  26.9 0.1 add.21.whole_ref
  26.9 0.0 copy-done
  27.0 0.0 copy-start.1
  27.0 1.1 %copy-done.1 = s32[1536,96]{0,1:T(8,128)S(1)} copy-done((s32[1536,96]{0,1:T(8,128)S(1)}, s32[1536,96]{0,1:T(8,128)}, u32[]{:S(2)}) %copy-start.1) | copy-done | bytes 589848
  28.0 10.7 %shard_map.89 = (f32[32,32,256]{2,1,0:T(8,128)S(1)}, f32[16,768]{1,0:T(8,128)}) custom-call(f32[128,896]{1,0:T(8,128)S(1)} %add.21.whole_ref, bf16[768,768]{1,0:T(8,128)(2,1)S(1)} %copy-done, f32[4,768,1536]{2,1,0:T(8,128)} %get-tuple-element.6.after_ref.rotated_hbm, s32[1,1536]{1,0:T(1,128)S(1)} %broadcast_in_dim.17.assign_ref, s32[96,1536]{1,0:T(8,128)S(1)} %bitcast.20), custom_call_target="tpu_custom_call" | custom-call | tf_op jit(solution)/shard_map/pallas_call | solution.py:328
  38.8 0.2 collective-permute-start.1
  39.0 1.8 %collective-permute-done.1 = f32[16,32,256]{2,1,0:T(8,128)S(1)} collective-permute-done((f32[16,32,256]{2,1,0:T(8,128)S(1)}, f32[16,32,256]{2,1,0:T(8,128)S(1)}, u32[]{:S(2)}, u32[]{:S(2)}) %collective-permute-start.1) | collective-permute-done | bytes 524320 | tf_op jit(solution)/shard_map/ppermute | solution.py:349
  40.7 0.1 fusion
  40.8 13.8 %all_to_all.15 = bf16[16,32,256]{2,1,0:T(8,128)(2,1)S(1)} all-to-all(bf16[16,32,256]{2,1,0:T(8,128)(2,1)S(1)} %fusion), channel_id=1, replica_groups=mesh['lists'=4,'z'=4,'core'=2] {'lists','z'}, dimensions={0} | all-to-all | bytes 524288 | tf_op jit(solution)/shard_map/all_to_all | solution.py:351
  54.7 11.6 %all_to_all.16 = bf16[16,24,256]{2,1,0:T(8,128)(2,1)S(1)} all-to-all(bf16[16,24,256]{2,1,0:T(8,128)(2,1)S(1)} %broadcast_in_dim.18), channel_id=1, replica_groups=mesh['lists'=4,'z'=4,'core'=2] {'lists','z'}, dimensions={0} | all-to-all | bytes 393216 | tf_op jit(solution)/shard_map/all_to_all | solution.py:357
  66.3 0.0 collective-permute-start.2
  66.3 1.4 %collective-permute-done.2 = bf16[384,256]{1,0:T(8,128)(2,1)S(1)} collective-permute-done((bf16[384,256]{1,0:T(8,128)(2,1)S(1)}, bf16[384,256]{1,0:T(8,128)(2,1)S(1)}, u32[]{:S(2)}, u32[]{:S(2)}) %collective-permute-start.2) | collective-permute-done | bytes 196640 | tf_op jit(solution)/shard_map/ppermute | solution.py:359
  67.8 0.9 %maximum_convert_fusion = f32[768,256]{1,0:T(8,128)} fusion(bf16[384,256]{1,0:T(8,128)(2,1)S(1)} %get-tuple-element.11, bf16[384,256]{1,0:T(8,128)(2,1)S(1)} %get-tuple-element.10), kind=kLoop, calls=%fused_computation.4 | loop fusion | flops 786432 | bytes 1179648 | tf_op jit(solution)/shard_map/convert_element_type | solution.py:362
  (7 shorter events, 0.2 us)
Async XLA Ops:
  2.6 21.7 %all-to-all-start = ((s16[16,16,768]{2,1,0:T(8,128)(2,1)}), s16[16,16,768]{2,1,0:T(8,128)(2,1)S(1)}, u32[]{:S(2)}, u32[]{:S(2)}) async-start(s16[16,16,768]{2,1,0:T(8,128)(2,1)} %bitcast.21), calls=%async_computation | async-start | bytes 786432 | tf_op jit(solution)/shard_map/all_to_all | solution.py:301
  24.3 0.7 %copy-start.2 = (s32[1536]{0:T(1024)S(1)}, s32[1536]{0:T(1024)}, u32[]{:S(2)}) copy-start(s32[1536]{0:T(1024)} %param.11) | copy-start | bytes 18436
  24.3 2.6 %copy-start = (bf16[768,768]{1,0:T(8,128)(2,1)S(1)}, bf16[768,768]{1,0:T(8,128)(2,1)}, u32[]{:S(2)}) copy-start(bf16[768,768]{1,0:T(8,128)(2,1)} %get-tuple-element.7.turned_hbm) | copy-start | bytes 3538948
  25.0 1.9 %collective-permute-start = (f32[128,896]{1,0:T(8,128)S(1)}, f32[128,896]{1,0:T(8,128)S(1)}, u32[]{:S(2)}, u32[]{:S(2)}) collective-permute-start(f32[128,896]{1,0:T(8,128)S(1)} %shard_map.88), channel_id=1, source_target_pairs={{0,1},{1,0},{2,3},{3,2},{4,5},{5,4},{6,7},{7,6},{8,9},{9,8},{10,11... | collective-permute-start | bytes 1376264 | tf_op jit(solution)/shard_map/ppermute | solution.py:325
  27.0 1.1 %copy-start.1 = (s32[1536,96]{0,1:T(8,128)S(1)}, s32[1536,96]{0,1:T(8,128)}, u32[]{:S(2)}) copy-start(s32[1536,96]{0,1:T(8,128)} %param.12) | copy-start | bytes 1769476
  38.8 2.0 %collective-permute-start.1 = (f32[16,32,256]{2,1,0:T(8,128)S(1)}, f32[16,32,256]{2,1,0:T(8,128)S(1)}, u32[]{:S(2)}, u32[]{:S(2)}) collective-permute-start(f32[16,32,256]{2,1,0:T(8,128)S(1)} %dynamic-slice_bitcast_fusion), channel_id=1, source_target_pairs={{0,1},{1,0},{2,3},{3,2},{4,5},{5,4},{6,7},{7,6},{8,9},{9,8},{10,11... | collective-permute-start | bytes 1572872 | tf_op jit(solution)/shard_map/ppermute | solution.py:349
  66.3 1.4 %collective-permute-start.2 = (bf16[384,256]{1,0:T(8,128)(2,1)S(1)}, bf16[384,256]{1,0:T(8,128)(2,1)S(1)}, u32[]{:S(2)}, u32[]{:S(2)}) collective-permute-start(bf16[384,256]{1,0:T(8,128)(2,1)S(1)} %bitcast.22), channel_id=1, source_target_pairs={{0,1},{1,0},{2,3},{3,2},{4,5},{5,4},{6,7},{7,6},{8,9},{9,8},{10,11... | collective-permute-start | bytes 589832 | tf_op jit(solution)/shard_map/ppermute | solution.py:359

commit v3 on v2

--- a/solution.py
+++ b/solution.py
@@ -18,7 +18,6 @@
 SIZE_BITS, PARENT_BITS, EXPONENT_BITS = 9, 13, 8
 SLABS = 4
 PIECES = 3
-BLOCKS = 2
 LANES = 128
 
 FULL = 66_900_000
@@ -117,72 +116,104 @@
     out_ref[:, width:] = picked(jnp.where(lane == 0, size, 0.0).astype(jnp.bfloat16))
 
 
-def rotate_kernel(points_hbm, rotation_hbm, out_hbm, turned_hbm, points_ref, rotation_ref, out_ref, turned_ref, in_sems, out_sems):
+def rotate_kernel(
+    points_hbm, points_other_hbm, codes_hbm, codes_other_hbm, assign_hbm, assign_other_hbm, rotation_hbm,
+    out_hbm, turned_hbm,
+    points_ref, codes_ref, assign_ref, rotation_ref, out_ref, turned_ref, note_ref, in_sems, out_sems,
+):
     width, count = out_ref.shape
-    piece, rows = count // PIECES, width // BLOCKS
-    fetch = pltpu.make_async_copy(rotation_hbm, rotation_ref, in_sems.at[PIECES])
+    own = count // 2
+    subspaces = codes_ref.shape[1] // 2
+    piece = own // PIECES
+    core = lax.axis_index("core")
+    first = pl.multiple_of(core * width, LANES)
+    fetch = pltpu.make_async_copy(rotation_hbm, rotation_ref, in_sems.at[0])
     fetch.start()
-    parts = [slice(step * piece, (step + 1) * piece) for step in range(PIECES)]
-    blocks = [slice(step * rows, (step + 1) * rows) for step in range(BLOCKS)]
-    fetches = [
-        pltpu.make_async_copy(points_hbm.at[part], points_ref.at[part], in_sems.at[k]) for k, part in enumerate(parts)
-    ]
-    for copy in fetches:
+    fetches = []
+    for side, source in enumerate((points_hbm, points_other_hbm)):
+        for k in range(PIECES):
+            part = slice(k * piece, (k + 1) * piece)
+            target = points_ref.at[side * own + k * piece : side * own + (k + 1) * piece]
+            fetches.append(pltpu.make_async_copy(source.at[part], target, in_sems.at[1 + side * PIECES + k]))
+    notes = []
+    for k, (source, target) in enumerate(
+        (
+            (codes_hbm, codes_ref.at[0]),
+            (codes_other_hbm, codes_ref.at[1]),
+            (assign_hbm, assign_ref.at[0]),
+            (assign_other_hbm, assign_ref.at[1]),
+        )
+    ):
+        notes.append(pltpu.make_async_copy(source, target, in_sems.at[1 + 2 * PIECES + k]))
+    for copy in fetches + notes:
         copy.start()
     fetch.wait()
-    turned_ref[...] = rotation_ref[...].T
-    stores = [pltpu.make_async_copy(turned_ref, turned_hbm, out_sems.at[PIECES * BLOCKS])]
+    turned_ref[...] = rotation_ref[:, pl.ds(first, width)].T
+    stores = [pltpu.make_async_copy(turned_ref, turned_hbm, out_sems.at[2 * PIECES])]
     stores[0].start()
-    for k, part in enumerate(parts):
+    for k in range(2 * PIECES):
+        part = slice(k * piece, (k + 1) * piece)
         fetches[k].wait()
-        for j, block in enumerate(blocks):
-            out_ref[block, part] = dot_nt(turned_ref[block, :], points_ref[part, :])
-            store = pltpu.make_async_copy(
-                out_ref.at[block, part], out_hbm.at[0, block, part], out_sems.at[k * BLOCKS + j]
-            )
-            store.start()
-            stores.append(store)
+        out_ref[:, part] = dot_nt(turned_ref[...], points_ref[part, :])
+        store = pltpu.make_async_copy(out_ref.at[:, part], out_hbm.at[0, :, part], out_sems.at[k])
+        store.start()
+        stores.append(store)
+    for copy in notes:
+        copy.wait()
+    chosen = pl.ds(pl.multiple_of(core * subspaces, 8), subspaces)
+    for side in range(2):
+        part = slice(side * own, (side + 1) * own)
+        code = codes_ref[side, chosen, :]
+        note_ref[:subspaces, part] = (code & (LOW - 1)).astype(jnp.float32)
+        note_ref[subspaces : 2 * subspaces, part] = (code // LOW).astype(jnp.float32)
+        note_ref[2 * subspaces :, part] = jnp.broadcast_to(assign_ref[side].astype(jnp.float32), (8, own))
+    store = pltpu.make_async_copy(note_ref, out_hbm.at[1, : 2 * subspaces + 8], out_sems.at[2 * PIECES + 1])
+    store.start()
+    stores.append(store)
     for store in stores:
         store.wait()
 
 
 def code_kernel(
-    whole_ref, turned_hbm, rotated_hbm, assign_ref, codes_ref,
-    out_ref, merged_ref, all_ref, rot_ref, pick_ref, turned_ref, sems,
+    whole_ref, turned_hbm, rotated_hbm, out_ref, merged_ref, all_ref, rot_ref, pick_ref, turned_ref, note_ref, sems
 ):
     width, count = rot_ref.shape
-    parents = all_ref.shape[0]
-    sub_width = width // codes_ref.shape[0]
-    steps = codes_ref.shape[0] // (SIDE * UNROLL)
+    parents, columns = all_ref.shape
+    subspaces = out_ref.shape[0] * GROUP
+    sub_width = width // subspaces
+    steps = subspaces // (SIDE * UNROLL)
     rows = width // steps
+    note = pltpu.make_async_copy(rotated_hbm.at[1, : 2 * subspaces + 8], note_ref, sems.at[steps + 1])
+    note.start()
     fetch = pltpu.make_async_copy(turned_hbm, turned_ref, sems.at[steps])
     fetch.start()
 
     def fetched(step):
-        span = pl.ds(pl.multiple_of(step * rows, rows), rows)
+        span = pl.ds(step * rows, rows)
         return pltpu.make_async_copy(rotated_hbm.at[0, span], rot_ref.at[span], sems.at[step])
 
     for step in range(steps):
         fetched(step).start()
-    all_ref[...] = whole_ref[:, :width] / whole_ref[:, width : width + 1]
+    all_ref[...] = whole_ref[:, :columns] / whole_ref[:, columns : columns + 1]
     shard_rows = merged_ref.shape[0]
     shard = lax.axis_index("z") * 2 + lax.axis_index("core")
     merged_ref[...] = all_ref[pl.ds(pl.multiple_of(shard * shard_rows, shard_rows), shard_rows), :]
     lowered = all_ref[...].astype(jnp.bfloat16)
-    ids = lax.broadcasted_iota(jnp.int32, (parents, count), 0)
-    pick = jnp.where(ids == assign_ref[...], 1.0, 0.0).astype(jnp.bfloat16)
+    note.wait()
+    ids = lax.broadcasted_iota(jnp.int32, (parents, count), 0).astype(jnp.float32)
+    pick = jnp.where(ids == note_ref[2 * subspaces : 2 * subspaces + 1, :], 1.0, 0.0).astype(jnp.bfloat16)
     pick_ref[:parents, :] = pick
     pick_ref[parents:, :] = pick
-    piece = count // PIECES
+    piece = count // (2 * PIECES)
 
     def correct(step):
-        span = pl.ds(pl.multiple_of(step * rows, rows), rows)
+        span = pl.ds(step * rows, rows)
         parent = dot_nt(turned_ref[span, :], lowered)
         upper = parent.astype(jnp.bfloat16)
         lower = (parent - upper.astype(jnp.float32)).astype(jnp.bfloat16)
         both = jnp.concatenate([upper, lower], axis=1)
         fetched(step).wait()
-        for k in range(PIECES):
+        for k in range(2 * PIECES):
             part = slice(k * piece, (k + 1) * piece)
             chosen = jnp.dot(both, pick_ref[:, part], preferred_element_type=jnp.float32)
             rot_ref[span, part] = rot_ref[span, part] - chosen
@@ -210,18 +241,17 @@
         weights, masked, highs = [], [], []
         for sub in range(SIDE):
             index = base + sub
-            code = codes_ref[pl.ds(index, 1), :]
-            low = small(jnp.broadcast_to(code & (LOW - 1), (tile, count)))
+            low = jnp.broadcast_to(note_ref[index : index + 1, :], (tile, count)).astype(jnp.bfloat16)
             weights += [jnp.where(ids == low, one, zero) for ids in low_ids]
-            value = rot_ref[pl.ds(pl.multiple_of(index * sub_width, sub_width), sub_width), :]
+            value = rot_ref[index * sub_width : (index + 1) * sub_width, :]
             value = jnp.concatenate([value, value], axis=0).astype(jnp.bfloat16)
-            high = jnp.broadcast_to(code // LOW, (tile, count))
+            high = jnp.broadcast_to(note_ref[subspaces + index : subspaces + index + 1, :], (tile, count))
             highs.append(high)
-            behind = small(high) - pair_ids
+            behind = high.astype(jnp.bfloat16) - pair_ids
             for k in range(0, HIGH, 2):
                 masked.append(jnp.where(behind == jnp.asarray(k, jnp.bfloat16), value, zero))
         for sub in range(0, SIDE, 2):
-            high = small(jnp.where(first_half, highs[sub], highs[sub + 1]))
+            high = jnp.where(first_half, highs[sub], highs[sub + 1]).astype(jnp.bfloat16)
             masked.append(jnp.where(high_ids == high, one, zero))
         result = dot_nt(jnp.concatenate(masked, axis=0), jnp.concatenate(weights, axis=0))
         sums, counts = [], []
@@ -259,7 +289,7 @@
             for place, sub in enumerate(mine):
                 row = jnp.broadcast_to(jnp.concatenate(counts[sub], axis=1), (8, CODEWORDS))
                 tally = jnp.where(wide_line == place, row, tally)
-            out_ref[step * (SIDE * UNROLL // GROUP) + k] = jnp.concatenate(lines + [tally], axis=0)
+            out_ref[step * (SIDE * UNROLL // GROUP) + k] = jnp.concatenate(lines + [tally], axis=0).astype(jnp.bfloat16)
 
 
 def whole(count):
@@ -299,22 +329,31 @@
         compiler_params=pltpu.CompilerParams(vmem_limit_bytes=FULL),
     )(child_centroids, child_sizes[None, :], parent_of[None, :])
     near = lax.all_to_all(packed.reshape(chips, most, width), ("lists", "z"), 0, 0)
+    half_width, half_subspaces, pair_count = width // 2, subspaces // 2, 2 * count
+    turned_codes, parent_row = codes.T, assign[None, :]
+
+    def both(array):
+        return array, lax.ppermute(array, "core", SWAP)
+
     rotated, turned = pl.pallas_call(
         rotate_kernel,
-        out_shape=(shaped((SLABS, width, count)), shaped((width, width), jnp.bfloat16)),
-        in_specs=anywhere(2),
+        out_shape=(shaped((SLABS, half_width, pair_count)), shaped((half_width, width), jnp.bfloat16)),
+        in_specs=anywhere(7),
         out_specs=tuple(anywhere(2)),
         scratch_shapes=[
-            pltpu.VMEM((count, width), jnp.bfloat16),
+            pltpu.VMEM((pair_count, width), jnp.bfloat16),
+            pltpu.VMEM((2, subspaces, count), jnp.int32),
+            pltpu.VMEM((2, 1, count), jnp.int32),
             pltpu.VMEM((width, width), jnp.bfloat16),
-            pltpu.VMEM((width, count), jnp.float32),
-            pltpu.VMEM((width, width), jnp.bfloat16),
-            pltpu.SemaphoreType.DMA((PIECES + 1,)),
-            pltpu.SemaphoreType.DMA((PIECES * BLOCKS + 1,)),
+            pltpu.VMEM((half_width, pair_count), jnp.float32),
+            pltpu.VMEM((half_width, width), jnp.bfloat16),
+            pltpu.VMEM((subspaces + 8, pair_count), jnp.float32),
+            pltpu.SemaphoreType.DMA((2 * PIECES + 5,)),
+            pltpu.SemaphoreType.DMA((2 * PIECES + 2,)),
         ],
         compiler_params=pltpu.CompilerParams(vmem_limit_bytes=MOST),
-        cost_estimate=pl.CostEstimate(flops=2 * width * width * count, bytes_accessed=10 << 20, transcendentals=0),
-    )(points, rotation)
+        cost_estimate=pl.CostEstimate(flops=2 * width * width * count, bytes_accessed=14 << 20, transcendentals=0),
+    )(*both(points), *both(turned_codes), *both(parent_row), rotation)
     mine = pl.pallas_call(
         merge_kernel,
         out_shape=shaped((owner_parents, wide)),
@@ -323,31 +362,27 @@
         compiler_params=pltpu.CompilerParams(vmem_limit_bytes=SOME),
     )(near.reshape(chips * most, width), rotated)
     sums_of_list = mine + lax.ppermute(mine, "core", SWAP)
-    groups = subspaces // GROUP
+    groups = half_subspaces // GROUP
     rows = GROUP * (width // subspaces) + 8
     sums, merged = pl.pallas_call(
         code_kernel,
-        out_shape=(shaped((groups, rows, CODEWORDS)), shaped((shard_rows, width))),
-        in_specs=whole(1) + anywhere(2) + whole(2),
+        out_shape=(shaped((groups, rows, CODEWORDS), jnp.bfloat16), shaped((shard_rows, width))),
+        in_specs=whole(1) + anywhere(2),
         out_specs=tuple(whole(2)),
         scratch_shapes=[
             pltpu.VMEM((owner_parents, width), jnp.float32),
-            pltpu.VMEM((width, count), jnp.float32),
-            pltpu.VMEM((2 * owner_parents, count), jnp.bfloat16),
-            pltpu.VMEM((width, width), jnp.bfloat16),
-            pltpu.SemaphoreType.DMA((subspaces // (SIDE * UNROLL) + 1,)),
+            pltpu.VMEM((half_width, pair_count), jnp.float32),
+            pltpu.VMEM((2 * owner_parents, pair_count), jnp.bfloat16),
+            pltpu.VMEM((half_width, width), jnp.bfloat16),
+            pltpu.VMEM((subspaces + 8, pair_count), jnp.float32),
+            pltpu.SemaphoreType.DMA((half_subspaces // (SIDE * UNROLL) + 2,)),
         ],
         compiler_params=pltpu.CompilerParams(vmem_limit_bytes=SOME),
-    )(sums_of_list, turned, rotated, assign[None, :], codes.T)
-
-    half_groups = groups // 2
-    splits = chips // half_groups
-    sums = sums.reshape(2, half_groups, rows, splits, CODEWORDS // splits)
-    sums = sums.transpose(0, 1, 3, 2, 4).reshape(2, chips, rows, CODEWORDS // splits)
-    kept = lax.dynamic_index_in_dim(sums, core, 0, keepdims=False)
-    given = lax.dynamic_index_in_dim(sums, 1 - core, 0, keepdims=False)
-    taken = lax.ppermute(given, "core", SWAP)
-    chip = (kept.astype(jnp.float32) + taken.astype(jnp.float32)).astype(jnp.bfloat16)
+    )(sums_of_list, turned, rotated)
+
+    splits = chips // groups
+    chip = sums.reshape(groups, rows, splits, CODEWORDS // splits)
+    chip = chip.transpose(0, 2, 1, 3).reshape(chips, rows, CODEWORDS // splits)
     total = jnp.sum(lax.all_to_all(chip, ("lists", "z"), 0, 0).astype(jnp.float32), axis=0)
     sub_width = (rows - 8) // GROUP
     tops = total[: rows - 8].reshape(GROUP, sub_width, -1)
@@ -355,7 +390,7 @@
     means = means.reshape(1, rows - 8, -1).astype(jnp.bfloat16)
     means = jnp.broadcast_to(means, (chips,) + means.shape[1:])
     mine = lax.all_to_all(means, ("lists", "z"), 0, 0)
-    mine = mine.reshape(half_groups, splits, rows - 8, -1).transpose(0, 2, 1, 3).reshape(-1, CODEWORDS)
+    mine = mine.reshape(groups, splits, rows - 8, -1).transpose(0, 2, 1, 3).reshape(-1, CODEWORDS)
     other = lax.ppermute(mine, "core", SWAP)
     first = core == 0
     means = jnp.concatenate([jnp.where(first, mine, other), jnp.where(first, other, mine)], axis=0)

time: 69.1 us -> 65.6 us (0.949)
  waiting for transfers between devices: 13.3 us -> 9.39 us
    all_to_all x1, waiting for transfers between devices: 8.3 us -> 4.98 us  [body(): lax.all_to_all(packed.reshape(chips, most, width), ('lists', 'z'), 0, 0)]
    broadcast_in_dim x1, local copies, waits for them, and re-layouts: 0.01 us -> 0.7 us  [body(): turned_codes, parent_row = (codes.T, assign[None, :])]
    ppermute x1 -> x3, waiting for transfers between devices: 1.77 us -> 1.17 us  [both(): return (array, lax.ppermute(array, 'core', SWAP))]
  transfers between devices with their start and end apart: 4 -> 6, of which waited for: 4 -> 4; matrix products, arithmetic and copies ran while one was open for 0% -> 1% of each run, Pallas kernels for 7% -> 12%
where the time goes in v3:
time: 65.6 us; the launch traced here: 65.2 us
  blocking collectives  25.3 us (39%)
  Pallas kernels  18.4 us (28%)
  waiting for transfers between devices  9.39 us (14%)
  starting transfers between devices  8.98 us (14%)
  local copies, waits for them, and re-layouts  1.3 us (2%)
  other arithmetic  1.09 us (2%)
  between operations  0.74 us (1%)
    all_to_all x1, blocking collectives, body(): lax.all_to_all(chip, ('lists', 'z'), 0, 0).astype(jnp.float32)  13.8 us
    all_to_all x1, blocking collectives, body(): mine = lax.all_to_all(means, ('lists', 'z'), 0, 0)  11.6 us
    pallas_call x1, Pallas kernels, body(): pl.pallas_call(code_kernel, out_shape=(shaped((groups, rows, CODEWORDS),...  9.56 us
    all_to_all x1, starting transfers between devices, body(): lax.all_to_all(packed.reshape(chips, most, width), ('lists', 'z'), 0, 0)  8.3 us
    pallas_call x1, Pallas kernels, body(): pl.pallas_call(rotate_kernel, out_shape=(shaped((SLABS, half_width, pair_...  6.17 us
    all_to_all x1, waiting for transfers between devices, body(): lax.all_to_all(packed.reshape(chips, most, width), ('lists', 'z'), 0, 0)  4.98 us
    pallas_call x1, Pallas kernels, body(): pl.pallas_call(functools.partial(pack_kernel, owner_parents), out_shape=s...  1.98 us
    ppermute x1, waiting for transfers between devices, body(): sums_of_list = mine + lax.ppermute(mine, 'core', SWAP)  1.8 us
  transfers between devices with their start and end apart: 6, of which 4 were waited for; matrix products, arithmetic and copies ran while one was open for 1% of the time, Pallas kernels for 12%

profile of v3, /device:TPU:0, one launch (start us, length us, event | category | flops | bytes accessed | tf_op | source)
XLA Modules:
  0.0 65.2 jit_solution(15045475815260213851)
XLA Ops:
  0.6 0.5 collective-permute-start
  1.1 0.1 collective-permute-start.1
  1.2 2.0 %shard_map.86 = s16[4,4,16,768]{3,2,1,0:T(8,128)(2,1)} custom-call(f32[32,768]{1,0:T(8,128)} %child_hbm.1, s32[1,32]{1,0:T(1,128)} %bitcast.15, s32[1,32]{1,0:T(1,128)} %bitcast.16), custom_call_target="tpu_custom_call" | custom-call | tf_op jit(solution)/shard_map/pallas_call | solution.py:318
  3.2 8.3 %all-to-all-start = ((s16[16,16,768]{2,1,0:T(8,128)(2,1)}), s16[16,16,768]{2,1,0:T(8,128)(2,1)S(1)}, u32[]{:S(2)}, u32[]{:S(2)}) async-start(s16[16,16,768]{2,1,0:T(8,128)(2,1)} %bitcast.11), calls=%async_computation | async-start | bytes 786432 | tf_op jit(solution)/shard_map/all_to_all | solution.py:331
  11.5 0.7 %broadcast_in_dim.17.assign_hbm = s32[1,1536]{1,0:T(1,128)S(1)} reshape(s32[1536]{0:T(1024)} %param.11) | data formatting | bytes 12288 | tf_op jit(solution)/shard_map/broadcast_in_dim | solution.py:333
  12.2 0.0 copy-start.1
  12.2 0.0 collective-permute-start.2
  12.2 1.2 %collective-permute-done.2.assign_other_hbm = s32[1,1536]{1,0:T(1,128)S(1)} collective-permute-done((s32[1,1536]{1,0:T(1,128)S(1)}, s32[1,1536]{1,0:T(1,128)S(1)}, u32[]{:S(2)}, u32[]{:S(2)}) %collective-permute-start.2) | collective-permute-done | bytes 6176 | tf_op jit(solution)/shard_map/ppermute | solution.py:336
  13.4 0.0 copy-start.2
  13.4 0.0 collective-permute-done.1.codes_other_hbm
  13.4 0.0 collective-permute-done.points_other_hbm
  13.4 0.0 copy-done.1
  13.4 0.6 copy-done.2
  14.0 6.2 %shard_map.87 = (f32[4,384,3072]{2,1,0:T(8,128)}, bf16[384,768]{1,0:T(8,128)(2,1)}) custom-call(bf16[1536,768]{1,0:T(8,128)(2,1)} %points_hbm.1, bf16[1536,768]{1,0:T(8,128)(2,1)} %collective-permute-done.points_other_hbm, s32[96,1536]{1,0:T(8,128)} %bitcast.14, s32[96,1536]{1,0:T(8,128)} %collective-permute-done.1.codes_other_hbm, s32[1,1536]{1,0:T(1,128)} %copy-done.1, ...), custom_call_target="tpu_custom_call" | custom-call | flops 1811939328 | bytes 14680064 | tf_op jit(solution)/shard_map/pallas_call | solution.py:338
  20.2 5.0 %all-to-all-done = s16[16,16,768]{2,1,0:T(8,128)(2,1)S(1)} async-done(((s16[16,16,768]{2,1,0:T(8,128)(2,1)}), s16[16,16,768]{2,1,0:T(8,128)(2,1)S(1)}, u32[]{:S(2)}, u32[]{:S(2)}) %all-to-all-start) | async-done | bytes 393248 | tf_op jit(solution)/shard_map/all_to_all | solution.py:331
  25.2 0.0 copy-start
  25.2 0.7 %shard_map.88 = f32[128,896]{1,0:T(8,128)S(1)} custom-call(s16[256,768]{1,0:T(8,128)(2,1)S(1)} %bitcast.10, f32[4,384,3072]{2,1,0:T(8,128)} %get-tuple-element.6.after_ref.rotated_hbm), custom_call_target="tpu_custom_call" | custom-call | tf_op jit(solution)/shard_map/pallas_call | solution.py:357
  25.8 0.1 collective-permute-start.3
  25.9 1.8 %collective-permute-done.3 = f32[128,896]{1,0:T(8,128)S(1)} collective-permute-done((f32[128,896]{1,0:T(8,128)S(1)}, f32[128,896]{1,0:T(8,128)S(1)}, u32[]{:S(2)}, u32[]{:S(2)}) %collective-permute-start.3) | collective-permute-done | bytes 458784 | tf_op jit(solution)/shard_map/ppermute | solution.py:364
  27.7 0.1 add.10.whole_ref
  27.7 0.0 copy-done
  27.8 9.6 %shard_map.89 = (bf16[16,32,256]{2,1,0:T(8,128)(2,1)S(1)}, f32[16,768]{1,0:T(8,128)}) custom-call(f32[128,896]{1,0:T(8,128)S(1)} %add.10.whole_ref, bf16[384,768]{1,0:T(8,128)(2,1)S(1)} %copy-done, f32[4,384,3072]{2,1,0:T(8,128)} %get-tuple-element.6.after_ref.rotated_hbm), custom_call_target="tpu_custom_call" | custom-call | tf_op jit(solution)/shard_map/pallas_call | solution.py:367
  37.3 13.8 %all_to_all.15 = bf16[16,32,256]{2,1,0:T(8,128)(2,1)S(1)} all-to-all(bf16[16,32,256]{2,1,0:T(8,128)(2,1)S(1)} %get-tuple-element.9), channel_id=1, replica_groups=mesh['lists'=4,'z'=4,'core'=2] {'lists','z'}, dimensions={0} | all-to-all | bytes 524288 | tf_op jit(solution)/shard_map/all_to_all | solution.py:386
  51.2 11.6 %all_to_all.16 = bf16[16,24,256]{2,1,0:T(8,128)(2,1)S(1)} all-to-all(bf16[16,24,256]{2,1,0:T(8,128)(2,1)S(1)} %broadcast_in_dim.18), channel_id=1, replica_groups=mesh['lists'=4,'z'=4,'core'=2] {'lists','z'}, dimensions={0} | all-to-all | bytes 393216 | tf_op jit(solution)/shard_map/all_to_all | solution.py:392
  62.8 0.0 collective-permute-start.4
  62.8 1.4 %collective-permute-done.4 = bf16[384,256]{1,0:T(8,128)(2,1)S(1)} collective-permute-done((bf16[384,256]{1,0:T(8,128)(2,1)S(1)}, bf16[384,256]{1,0:T(8,128)(2,1)S(1)}, u32[]{:S(2)}, u32[]{:S(2)}) %collective-permute-start.4) | collective-permute-done | bytes 196640 | tf_op jit(solution)/shard_map/ppermute | solution.py:394
  64.3 0.9 %maximum_convert_fusion = f32[768,256]{1,0:T(8,128)} fusion(bf16[384,256]{1,0:T(8,128)(2,1)S(1)} %get-tuple-element.11, bf16[384,256]{1,0:T(8,128)(2,1)S(1)} %get-tuple-element.10), kind=kLoop, calls=%fused_computation.1 | loop fusion | flops 786432 | bytes 1179648 | tf_op jit(solution)/shard_map/convert_element_type | solution.py:397
  (5 shorter events, 0.1 us)
Async XLA Ops:
  0.6 12.8 %collective-permute-start = (bf16[1536,768]{1,0:T(8,128)(2,1)}, bf16[1536,768]{1,0:T(8,128)(2,1)}, u32[]{:S(2)}, u32[]{:S(2)}) collective-permute-start(bf16[1536,768]{1,0:T(8,128)(2,1)} %points_hbm.1), channel_id=1, source_target_pairs={{0,1},{1,0},{2,3},{3,2},{4,5},{5,4},{6,7},{7,6},{8,9},{9,8},{10,11... | collective-permute-start | bytes 7077896 | tf_op jit(solution)/shard_map/ppermute | solution.py:336
  1.1 12.3 %collective-permute-start.1 = (s32[96,1536]{1,0:T(8,128)}, s32[96,1536]{1,0:T(8,128)}, u32[]{:S(2)}, u32[]{:S(2)}) collective-permute-start(s32[96,1536]{1,0:T(8,128)} %bitcast.13), channel_id=1, source_target_pairs={{0,1},{1,0},{2,3},{3,2},{4,5},{5,4},{6,7},{7,6},{8,9},{9,8},{10,11... | collective-permute-start | bytes 1769480 | tf_op jit(solution)/shard_map/ppermute | solution.py:336
  3.2 21.9 %all-to-all-start = ((s16[16,16,768]{2,1,0:T(8,128)(2,1)}), s16[16,16,768]{2,1,0:T(8,128)(2,1)S(1)}, u32[]{:S(2)}, u32[]{:S(2)}) async-start(s16[16,16,768]{2,1,0:T(8,128)(2,1)} %bitcast.11), calls=%async_computation | async-start | bytes 786432 | tf_op jit(solution)/shard_map/all_to_all | solution.py:331
  12.2 1.2 %copy-start.1 = (s32[1,1536]{1,0:T(1,128)}, s32[1,1536]{1,0:T(1,128)S(1)}, u32[]{:S(2)}) copy-start(s32[1,1536]{1,0:T(1,128)S(1)} %broadcast_in_dim.17.assign_hbm) | copy-start | bytes 18436
  12.2 1.2 %collective-permute-start.2 = (s32[1,1536]{1,0:T(1,128)S(1)}, s32[1,1536]{1,0:T(1,128)S(1)}, u32[]{:S(2)}, u32[]{:S(2)}) collective-permute-start(s32[1,1536]{1,0:T(1,128)S(1)} %broadcast_in_dim.17.assign_hbm), channel_id=1, source_target_pairs={{0,1},{1,0},{2,3},{3,2},{4,5},{5,4},{6,7},{7,6},{8,9},{9,8},{10,11... | collective-permute-start | bytes 18440 | tf_op jit(solution)/shard_map/ppermute | solution.py:336
  13.4 0.6 copy-start.2
  25.2 2.6 %copy-start = (bf16[384,768]{1,0:T(8,128)(2,1)S(1)}, bf16[384,768]{1,0:T(8,128)(2,1)}, u32[]{:S(2)}) copy-start(bf16[384,768]{1,0:T(8,128)(2,1)} %get-tuple-element.7.turned_hbm) | copy-start | bytes 1769476
  25.8 1.9 %collective-permute-start.3 = (f32[128,896]{1,0:T(8,128)S(1)}, f32[128,896]{1,0:T(8,128)S(1)}, u32[]{:S(2)}, u32[]{:S(2)}) collective-permute-start(f32[128,896]{1,0:T(8,128)S(1)} %shard_map.88), channel_id=1, source_target_pairs={{0,1},{1,0},{2,3},{3,2},{4,5},{5,4},{6,7},{7,6},{8,9},{9,8},{10,11... | collective-permute-start | bytes 1376264 | tf_op jit(solution)/shard_map/ppermute | solution.py:364
  62.8 1.4 %collective-permute-start.4 = (bf16[384,256]{1,0:T(8,128)(2,1)S(1)}, bf16[384,256]{1,0:T(8,128)(2,1)S(1)}, u32[]{:S(2)}, u32[]{:S(2)}) collective-permute-start(bf16[384,256]{1,0:T(8,128)(2,1)S(1)} %bitcast.12), channel_id=1, source_target_pairs={{0,1},{1,0},{2,3},{3,2},{4,5},{5,4},{6,7},{7,6},{8,9},{9,8},{10,11... | collective-permute-start | bytes 589832 | tf_op jit(solution)/shard_map/ppermute | solution.py:394

commit v4 on v3

--- a/solution.py
+++ b/solution.py
@@ -13,7 +13,7 @@
 HIGH = CODEWORDS // LOW
 GROUP = 3
 SIDE = 8
-UNROLL = 3
+SHARES = (2, 4)
 FRACTION = 14.0
 SIZE_BITS, PARENT_BITS, EXPONENT_BITS = 9, 13, 8
 SLABS = 4
@@ -118,7 +118,7 @@
 
 def rotate_kernel(
     points_hbm, points_other_hbm, codes_hbm, codes_other_hbm, assign_hbm, assign_other_hbm, rotation_hbm,
-    out_hbm, turned_hbm,
+    out_hbm, early_hbm, turned_hbm,
     points_ref, codes_ref, assign_ref, rotation_ref, out_ref, turned_ref, note_ref, in_sems, out_sems,
 ):
     width, count = out_ref.shape
@@ -149,74 +149,97 @@
         copy.start()
     fetch.wait()
     turned_ref[...] = rotation_ref[:, pl.ds(first, width)].T
-    stores = [pltpu.make_async_copy(turned_ref, turned_hbm, out_sems.at[2 * PIECES])]
+    early = SHARES[0] * SIDE * (width // subspaces)
+    stores = [pltpu.make_async_copy(turned_ref, turned_hbm, out_sems.at[4 * PIECES])]
     stores[0].start()
     for k in range(2 * PIECES):
         part = slice(k * piece, (k + 1) * piece)
         fetches[k].wait()
         out_ref[:, part] = dot_nt(turned_ref[...], points_ref[part, :])
-        store = pltpu.make_async_copy(out_ref.at[:, part], out_hbm.at[0, :, part], out_sems.at[k])
-        store.start()
-        stores.append(store)
+        for j, (source, target) in enumerate(
+            (
+                (out_ref.at[:early, part], early_hbm.at[:early, part]),
+                (out_ref.at[early:, part], out_hbm.at[0, early:, part]),
+            )
+        ):
+            store = pltpu.make_async_copy(source, target, out_sems.at[2 * k + j])
+            store.start()
+            stores.append(store)
     for copy in notes:
         copy.wait()
     chosen = pl.ds(pl.multiple_of(core * subspaces, 8), subspaces)
     for side in range(2):
         part = slice(side * own, (side + 1) * own)
         code = codes_ref[side, chosen, :]
-        note_ref[:subspaces, part] = (code & (LOW - 1)).astype(jnp.float32)
-        note_ref[subspaces : 2 * subspaces, part] = (code // LOW).astype(jnp.float32)
+        low, high = (code & (LOW - 1)).astype(jnp.float32), (code // LOW).astype(jnp.float32)
+        for start in range(0, subspaces, SIDE):
+            note_ref[2 * start : 2 * start + SIDE, part] = low[start : start + SIDE]
+            note_ref[2 * start + SIDE : 2 * (start + SIDE), part] = high[start : start + SIDE]
         note_ref[2 * subspaces :, part] = jnp.broadcast_to(assign_ref[side].astype(jnp.float32), (8, own))
-    store = pltpu.make_async_copy(note_ref, out_hbm.at[1, : 2 * subspaces + 8], out_sems.at[2 * PIECES + 1])
-    store.start()
-    stores.append(store)
+    lines, after = 2 * SHARES[0] * SIDE, 2 * subspaces
+    for k, (source, target) in enumerate(
+        (
+            (note_ref.at[:lines], early_hbm.at[early : early + lines]),
+            (note_ref.at[after:], early_hbm.at[early + lines :]),
+            (note_ref.at[lines:after], out_hbm.at[1, lines:after]),
+        )
+    ):
+        store = pltpu.make_async_copy(source, target, out_sems.at[4 * PIECES + 1 + k])
+        store.start()
+        stores.append(store)
     for store in stores:
         store.wait()
 
 
 def code_kernel(
-    whole_ref, turned_hbm, rotated_hbm, out_ref, merged_ref, all_ref, rot_ref, pick_ref, turned_ref, note_ref, sems
+    whole_ref, early_ref, turned_ref, rotated_hbm, out_ref, merged_hbm, all_ref, rot_ref, pick_ref, note_ref, sems
 ):
     width, count = rot_ref.shape
     parents, columns = all_ref.shape
     subspaces = out_ref.shape[0] * GROUP
     sub_width = width // subspaces
-    steps = subspaces // (SIDE * UNROLL)
-    rows = width // steps
-    note = pltpu.make_async_copy(rotated_hbm.at[1, : 2 * subspaces + 8], note_ref, sems.at[steps + 1])
-    note.start()
-    fetch = pltpu.make_async_copy(turned_hbm, turned_ref, sems.at[steps])
-    fetch.start()
-
-    def fetched(step):
-        span = pl.ds(step * rows, rows)
-        return pltpu.make_async_copy(rotated_hbm.at[0, span], rot_ref.at[span], sems.at[step])
-
-    for step in range(steps):
-        fetched(step).start()
+    shares = len(SHARES)
+    ends = [sum(SHARES[: k + 1]) * SIDE for k in range(shares)]
+    starts = [0] + ends[:-1]
+    early = ends[0] * sub_width
+
+    def columns_of(share):
+        return slice(starts[share] * sub_width, ends[share] * sub_width)
+
+    fetches, notes = [None], [None]
+    for share in range(1, shares):
+        span = columns_of(share)
+        fetches.append(pltpu.make_async_copy(rotated_hbm.at[0, span], rot_ref.at[span], sems.at[share]))
+        span = slice(2 * starts[share], 2 * ends[share])
+        notes.append(pltpu.make_async_copy(rotated_hbm.at[1, span], note_ref.at[span], sems.at[shares + share]))
+        fetches[share].start()
+        notes[share].start()
     all_ref[...] = whole_ref[:, :columns] / whole_ref[:, columns : columns + 1]
-    shard_rows = merged_ref.shape[0]
+    shard_rows = merged_hbm.shape[0]
     shard = lax.axis_index("z") * 2 + lax.axis_index("core")
-    merged_ref[...] = all_ref[pl.ds(pl.multiple_of(shard * shard_rows, shard_rows), shard_rows), :]
+    mine = all_ref.at[pl.ds(pl.multiple_of(shard * shard_rows, shard_rows), shard_rows)]
+    store = pltpu.make_async_copy(mine, merged_hbm, sems.at[0])
+    store.start()
     lowered = all_ref[...].astype(jnp.bfloat16)
-    note.wait()
     ids = lax.broadcasted_iota(jnp.int32, (parents, count), 0).astype(jnp.float32)
-    pick = jnp.where(ids == note_ref[2 * subspaces : 2 * subspaces + 1, :], 1.0, 0.0).astype(jnp.bfloat16)
+    pick = jnp.where(ids == early_ref[early + 2 * ends[0] : early + 2 * ends[0] + 1, :], 1.0, 0.0).astype(jnp.bfloat16)
     pick_ref[:parents, :] = pick
     pick_ref[parents:, :] = pick
     piece = count // (2 * PIECES)
 
-    def correct(step):
-        span = pl.ds(step * rows, rows)
+    def correct(share):
+        span = columns_of(share)
         parent = dot_nt(turned_ref[span, :], lowered)
         upper = parent.astype(jnp.bfloat16)
         lower = (parent - upper.astype(jnp.float32)).astype(jnp.bfloat16)
         both = jnp.concatenate([upper, lower], axis=1)
-        fetched(step).wait()
+        if share:
+            fetches[share].wait()
+        source = rot_ref if share else early_ref
         for k in range(2 * PIECES):
             part = slice(k * piece, (k + 1) * piece)
             chosen = jnp.dot(both, pick_ref[:, part], preferred_element_type=jnp.float32)
-            rot_ref[span, part] = rot_ref[span, part] - chosen
+            rot_ref[span, part] = source[span, part] - chosen
 
     def small(ids):
         return ids.astype(jnp.float32).astype(jnp.bfloat16)
@@ -239,13 +262,14 @@
 
     def spread(base):
         weights, masked, highs = [], [], []
+        note = note_ref if base >= ends[0] else early_ref.at[early:]
         for sub in range(SIDE):
             index = base + sub
-            low = jnp.broadcast_to(note_ref[index : index + 1, :], (tile, count)).astype(jnp.bfloat16)
+            low = jnp.broadcast_to(note[2 * base + sub : 2 * base + sub + 1, :], (tile, count)).astype(jnp.bfloat16)
             weights += [jnp.where(ids == low, one, zero) for ids in low_ids]
             value = rot_ref[index * sub_width : (index + 1) * sub_width, :]
             value = jnp.concatenate([value, value], axis=0).astype(jnp.bfloat16)
-            high = jnp.broadcast_to(note_ref[subspaces + index : subspaces + index + 1, :], (tile, count))
+            high = jnp.broadcast_to(note[2 * base + SIDE + sub : 2 * base + SIDE + sub + 1, :], (tile, count))
             highs.append(high)
             behind = high.astype(jnp.bfloat16) - pair_ids
             for k in range(0, HIGH, 2):
@@ -254,7 +278,7 @@
             high = jnp.where(first_half, highs[sub], highs[sub + 1]).astype(jnp.bfloat16)
             masked.append(jnp.where(high_ids == high, one, zero))
         result = dot_nt(jnp.concatenate(masked, axis=0), jnp.concatenate(weights, axis=0))
-        sums, counts = [], []
+        found = []
         for sub in range(SIDE):
             start = sub * HIGH * sub_width
             tally = result[SIDE * HIGH * sub_width + sub * HIGH :][:HIGH]
@@ -268,28 +292,25 @@
                     counted = piece if counted is None else jnp.where(spot == k % spots, piece, counted)
                 halves.append(total)
                 tallies.append(jnp.sum(counted, axis=0, keepdims=True))
-            sums.append(halves)
-            counts.append(tallies)
-        return sums, counts
-
-    fetch.wait()
-    correct(0)
-    for step in range(steps):
-        if step + 1 < steps:
-            correct(step + 1)
-        sums, counts = [], []
-        for k in range(UNROLL):
-            more_sums, more_counts = spread((step * UNROLL + k) * SIDE)
-            sums += more_sums
-            counts += more_counts
-        for k in range(SIDE * UNROLL // GROUP):
-            mine = range(k * GROUP, (k + 1) * GROUP)
-            lines = [jnp.concatenate(sums[sub], axis=1) for sub in mine]
-            tally = jnp.zeros((8, CODEWORDS), jnp.float32)
-            for place, sub in enumerate(mine):
-                row = jnp.broadcast_to(jnp.concatenate(counts[sub], axis=1), (8, CODEWORDS))
-                tally = jnp.where(wide_line == place, row, tally)
-            out_ref[step * (SIDE * UNROLL // GROUP) + k] = jnp.concatenate(lines + [tally], axis=0).astype(jnp.bfloat16)
+            found.append((halves, tallies))
+        return found
+
+    pending, done = [], 0
+    for share in range(shares):
+        if share:
+            notes[share].wait()
+        correct(share)
+        for base in range(starts[share], ends[share], SIDE):
+            pending += spread(base)
+            while len(pending) >= GROUP:
+                lines = [jnp.concatenate(halves, axis=1) for halves, _ in pending[:GROUP]]
+                tally = jnp.zeros((8, CODEWORDS), jnp.float32)
+                for place, (_, tallies) in enumerate(pending[:GROUP]):
+                    row = jnp.broadcast_to(jnp.concatenate(tallies, axis=1), (8, CODEWORDS))
+                    tally = jnp.where(wide_line == place, row, tally)
+                out_ref[done] = jnp.concatenate(lines + [tally], axis=0).astype(jnp.bfloat16)
+                pending, done = pending[GROUP:], done + 1
+    store.wait()
 
 
 def whole(count):
@@ -335,11 +356,17 @@
     def both(array):
         return array, lax.ppermute(array, "core", SWAP)
 
-    rotated, turned = pl.pallas_call(
+    first = SHARES[0] * SIDE
+    early_rows = first * (width // subspaces) + 2 * first + 8
+    rotated, early, turned = pl.pallas_call(
         rotate_kernel,
-        out_shape=(shaped((SLABS, half_width, pair_count)), shaped((half_width, width), jnp.bfloat16)),
+        out_shape=(
+            shaped((SLABS, half_width, pair_count)),
+            shaped((early_rows, pair_count)),
+            shaped((half_width, width), jnp.bfloat16),
+        ),
         in_specs=anywhere(7),
-        out_specs=tuple(anywhere(2)),
+        out_specs=tuple(anywhere(3)),
         scratch_shapes=[
             pltpu.VMEM((pair_count, width), jnp.bfloat16),
             pltpu.VMEM((2, subspaces, count), jnp.int32),
@@ -349,7 +376,7 @@
             pltpu.VMEM((half_width, width), jnp.bfloat16),
             pltpu.VMEM((subspaces + 8, pair_count), jnp.float32),
             pltpu.SemaphoreType.DMA((2 * PIECES + 5,)),
-            pltpu.SemaphoreType.DMA((2 * PIECES + 2,)),
+            pltpu.SemaphoreType.DMA((4 * PIECES + 4,)),
         ],
         compiler_params=pltpu.CompilerParams(vmem_limit_bytes=MOST),
         cost_estimate=pl.CostEstimate(flops=2 * width * width * count, bytes_accessed=14 << 20, transcendentals=0),
@@ -367,18 +394,17 @@
     sums, merged = pl.pallas_call(
         code_kernel,
         out_shape=(shaped((groups, rows, CODEWORDS), jnp.bfloat16), shaped((shard_rows, width))),
-        in_specs=whole(1) + anywhere(2),
-        out_specs=tuple(whole(2)),
+        in_specs=whole(3) + anywhere(1),
+        out_specs=tuple(whole(1) + anywhere(1)),
         scratch_shapes=[
             pltpu.VMEM((owner_parents, width), jnp.float32),
             pltpu.VMEM((half_width, pair_count), jnp.float32),
             pltpu.VMEM((2 * owner_parents, pair_count), jnp.bfloat16),
-            pltpu.VMEM((half_width, width), jnp.bfloat16),
             pltpu.VMEM((subspaces + 8, pair_count), jnp.float32),
-            pltpu.SemaphoreType.DMA((half_subspaces // (SIDE * UNROLL) + 2,)),
+            pltpu.SemaphoreType.DMA((2 * len(SHARES),)),
         ],
         compiler_params=pltpu.CompilerParams(vmem_limit_bytes=SOME),
-    )(sums_of_list, turned, rotated)
+    )(sums_of_list, early, turned, rotated)
 
     splits = chips // groups
     chip = sums.reshape(groups, rows, splits, CODEWORDS // splits)

time: 65.6 us -> 63.5 us (0.968)
  Pallas kernels: 18.4 us -> 16.4 us
    pallas_call x1, Pallas kernels: 9.56 us -> 7.49 us  [body(): pl.pallas_call(code_kernel, out_shape=(shaped((groups, rows, CODEWORDS),...]
  transfers between devices with their start and end apart: 6 -> 6, of which waited for: 4 -> 4; matrix products, arithmetic and copies ran while one was open for 1% -> 1% of each run, Pallas kernels for 12% -> 13%
where the time goes in v4:
time: 63.5 us; the launch traced here: 63.2 us
  blocking collectives  25.4 us (40%)
  Pallas kernels  16.4 us (26%)
  waiting for transfers between devices  9.33 us (15%)
  starting transfers between devices  8.98 us (14%)
  local copies, waits for them, and re-layouts  1.31 us (2%)
  other arithmetic  1.09 us (2%)
  between operations  0.74 us (1%)
    all_to_all x1, blocking collectives, body(): lax.all_to_all(chip, ('lists', 'z'), 0, 0).astype(jnp.float32)  13.8 us
    all_to_all x1, blocking collectives, body(): mine = lax.all_to_all(means, ('lists', 'z'), 0, 0)  11.6 us
    all_to_all x1, starting transfers between devices, body(): lax.all_to_all(packed.reshape(chips, most, width), ('lists', 'z'), 0, 0)  8.3 us
    pallas_call x1, Pallas kernels, body(): pl.pallas_call(code_kernel, out_shape=(shaped((groups, rows, CODEWORDS),...  7.49 us
    pallas_call x1, Pallas kernels, body(): pl.pallas_call(rotate_kernel, out_shape=(shaped((SLABS, half_width, pair_...  6.23 us
    all_to_all x1, waiting for transfers between devices, body(): lax.all_to_all(packed.reshape(chips, most, width), ('lists', 'z'), 0, 0)  4.92 us
    pallas_call x1, Pallas kernels, body(): pl.pallas_call(functools.partial(pack_kernel, owner_parents), out_shape=s...  1.99 us
    ppermute x1, waiting for transfers between devices, body(): sums_of_list = mine + lax.ppermute(mine, 'core', SWAP)  1.8 us
  transfers between devices with their start and end apart: 6, of which 4 were waited for; matrix products, arithmetic and copies ran while one was open for 1% of the time, Pallas kernels for 13%

profile of v4, /device:TPU:0, one launch (start us, length us, event | category | flops | bytes accessed | tf_op | source)
XLA Modules:
  0.0 63.2 jit_solution(913816894554358224)
XLA Ops:
  0.6 0.5 collective-permute-start
  1.1 0.1 collective-permute-start.1
  1.2 2.0 %shard_map.86 = s16[4,4,16,768]{3,2,1,0:T(8,128)(2,1)} custom-call(f32[32,768]{1,0:T(8,128)} %child_hbm.1, s32[1,32]{1,0:T(1,128)} %bitcast.15, s32[1,32]{1,0:T(1,128)} %bitcast.16), custom_call_target="tpu_custom_call" | custom-call | tf_op jit(solution)/shard_map/pallas_call | solution.py:339
  3.2 8.3 %all-to-all-start = ((s16[16,16,768]{2,1,0:T(8,128)(2,1)}), s16[16,16,768]{2,1,0:T(8,128)(2,1)S(1)}, u32[]{:S(2)}, u32[]{:S(2)}) async-start(s16[16,16,768]{2,1,0:T(8,128)(2,1)} %bitcast.11), calls=%async_computation | async-start | bytes 786432 | tf_op jit(solution)/shard_map/all_to_all | solution.py:352
  11.5 0.7 %broadcast_in_dim.17.assign_hbm = s32[1,1536]{1,0:T(1,128)S(1)} reshape(s32[1536]{0:T(1024)} %param.11) | data formatting | bytes 12288 | tf_op jit(solution)/shard_map/broadcast_in_dim | solution.py:354
  12.2 0.0 copy-start.2
  12.2 0.0 collective-permute-start.2
  12.3 1.2 %collective-permute-done.2.assign_other_hbm = s32[1,1536]{1,0:T(1,128)S(1)} collective-permute-done((s32[1,1536]{1,0:T(1,128)S(1)}, s32[1,1536]{1,0:T(1,128)S(1)}, u32[]{:S(2)}, u32[]{:S(2)}) %collective-permute-start.2) | collective-permute-done | bytes 6176 | tf_op jit(solution)/shard_map/ppermute | solution.py:357
  13.4 0.0 copy-start.3
  13.4 0.0 collective-permute-done.1.codes_other_hbm
  13.4 0.0 collective-permute-done.points_other_hbm
  13.4 0.0 copy-done.2
  13.4 0.6 copy-done.3
  14.0 6.2 %shard_map.87 = (f32[4,384,3072]{2,1,0:T(8,128)}, f32[168,3072]{1,0:T(8,128)}, bf16[384,768]{1,0:T(8,128)(2,1)}) custom-call(bf16[1536,768]{1,0:T(8,128)(2,1)} %points_hbm.1, bf16[1536,768]{1,0:T(8,128)(2,1)} %collective-permute-done.points_other_hbm, s32[96,1536]{1,0:T(8,128)} %bitcast.14, s32[96,1536]{1,0:T(8,128)} %collective-permute-done.1.codes_other_hbm, ...), custom_call_target="tpu_custom_call" | custom-call | flops 1811939328 | bytes 14680064 | tf_op jit(solution)/shard_map/pallas_call | solution.py:361
  20.2 4.9 %all-to-all-done = s16[16,16,768]{2,1,0:T(8,128)(2,1)S(1)} async-done(((s16[16,16,768]{2,1,0:T(8,128)(2,1)}), s16[16,16,768]{2,1,0:T(8,128)(2,1)S(1)}, u32[]{:S(2)}, u32[]{:S(2)}) %all-to-all-start) | async-done | bytes 393248 | tf_op jit(solution)/shard_map/all_to_all | solution.py:352
  25.2 0.0 copy-start
  25.2 0.0 copy-start.1
  25.2 0.7 %shard_map.88 = f32[128,896]{1,0:T(8,128)S(1)} custom-call(s16[256,768]{1,0:T(8,128)(2,1)S(1)} %bitcast.10, f32[4,384,3072]{2,1,0:T(8,128)} %get-tuple-element.7.after_ref.rotated_hbm), custom_call_target="tpu_custom_call" | custom-call | tf_op jit(solution)/shard_map/pallas_call | solution.py:384
  25.8 0.1 collective-permute-start.3
  25.9 1.8 %collective-permute-done.3 = f32[128,896]{1,0:T(8,128)S(1)} collective-permute-done((f32[128,896]{1,0:T(8,128)S(1)}, f32[128,896]{1,0:T(8,128)S(1)}, u32[]{:S(2)}, u32[]{:S(2)}) %collective-permute-start.3) | collective-permute-done | bytes 458784 | tf_op jit(solution)/shard_map/ppermute | solution.py:391
  27.7 0.1 add.10.whole_ref
  27.8 0.0 copy-done
  27.8 0.0 copy-done.1
  27.8 7.5 %shard_map.89 = (bf16[16,32,256]{2,1,0:T(8,128)(2,1)S(1)}, f32[16,768]{1,0:T(8,128)}) custom-call(f32[128,896]{1,0:T(8,128)S(1)} %add.10.whole_ref, f32[168,3072]{1,0:T(8,128)S(1)} %copy-done, bf16[384,768]{1,0:T(8,128)(2,1)S(1)} %copy-done.1, f32[4,384,3072]{2,1,0:T(8,128)} %get-tuple-element.7.after_ref.rotated_hbm), custom_call_target="tpu_custom_call" | custom-call | tf_op jit(solution)/shard_map/pallas_call | solution.py:394
  35.3 13.8 %all_to_all.15 = bf16[16,32,256]{2,1,0:T(8,128)(2,1)S(1)} all-to-all(bf16[16,32,256]{2,1,0:T(8,128)(2,1)S(1)} %get-tuple-element.11), channel_id=1, replica_groups=mesh['lists'=4,'z'=4,'core'=2] {'lists','z'}, dimensions={0} | all-to-all | bytes 524288 | tf_op jit(solution)/shard_map/all_to_all | solution.py:412
  49.1 11.6 %all_to_all.16 = bf16[16,24,256]{2,1,0:T(8,128)(2,1)S(1)} all-to-all(bf16[16,24,256]{2,1,0:T(8,128)(2,1)S(1)} %broadcast_in_dim.18), channel_id=1, replica_groups=mesh['lists'=4,'z'=4,'core'=2] {'lists','z'}, dimensions={0} | all-to-all | bytes 393216 | tf_op jit(solution)/shard_map/all_to_all | solution.py:418
  60.7 0.0 collective-permute-start.4
  60.7 1.4 %collective-permute-done.4 = bf16[384,256]{1,0:T(8,128)(2,1)S(1)} collective-permute-done((bf16[384,256]{1,0:T(8,128)(2,1)S(1)}, bf16[384,256]{1,0:T(8,128)(2,1)S(1)}, u32[]{:S(2)}, u32[]{:S(2)}) %collective-permute-start.4) | collective-permute-done | bytes 196640 | tf_op jit(solution)/shard_map/ppermute | solution.py:420
  62.2 0.9 %maximum_convert_fusion = f32[768,256]{1,0:T(8,128)} fusion(bf16[384,256]{1,0:T(8,128)(2,1)S(1)} %get-tuple-element.13, bf16[384,256]{1,0:T(8,128)(2,1)S(1)} %get-tuple-element.12), kind=kLoop, calls=%fused_computation.1 | loop fusion | flops 786432 | bytes 1179648 | tf_op jit(solution)/shard_map/convert_element_type | solution.py:423
  (5 shorter events, 0.1 us)
Async XLA Ops:
  0.6 12.8 %collective-permute-start = (bf16[1536,768]{1,0:T(8,128)(2,1)}, bf16[1536,768]{1,0:T(8,128)(2,1)}, u32[]{:S(2)}, u32[]{:S(2)}) collective-permute-start(bf16[1536,768]{1,0:T(8,128)(2,1)} %points_hbm.1), channel_id=1, source_target_pairs={{0,1},{1,0},{2,3},{3,2},{4,5},{5,4},{6,7},{7,6},{8,9},{9,8},{10,11... | collective-permute-start | bytes 7077896 | tf_op jit(solution)/shard_map/ppermute | solution.py:357
  1.1 12.3 %collective-permute-start.1 = (s32[96,1536]{1,0:T(8,128)}, s32[96,1536]{1,0:T(8,128)}, u32[]{:S(2)}, u32[]{:S(2)}) collective-permute-start(s32[96,1536]{1,0:T(8,128)} %bitcast.13), channel_id=1, source_target_pairs={{0,1},{1,0},{2,3},{3,2},{4,5},{5,4},{6,7},{7,6},{8,9},{9,8},{10,11... | collective-permute-start | bytes 1769480 | tf_op jit(solution)/shard_map/ppermute | solution.py:357
  3.2 21.9 %all-to-all-start = ((s16[16,16,768]{2,1,0:T(8,128)(2,1)}), s16[16,16,768]{2,1,0:T(8,128)(2,1)S(1)}, u32[]{:S(2)}, u32[]{:S(2)}) async-start(s16[16,16,768]{2,1,0:T(8,128)(2,1)} %bitcast.11), calls=%async_computation | async-start | bytes 786432 | tf_op jit(solution)/shard_map/all_to_all | solution.py:352
  12.2 1.2 %copy-start.2 = (s32[1,1536]{1,0:T(1,128)}, s32[1,1536]{1,0:T(1,128)S(1)}, u32[]{:S(2)}) copy-start(s32[1,1536]{1,0:T(1,128)S(1)} %broadcast_in_dim.17.assign_hbm) | copy-start | bytes 18436
  12.2 1.2 %collective-permute-start.2 = (s32[1,1536]{1,0:T(1,128)S(1)}, s32[1,1536]{1,0:T(1,128)S(1)}, u32[]{:S(2)}, u32[]{:S(2)}) collective-permute-start(s32[1,1536]{1,0:T(1,128)S(1)} %broadcast_in_dim.17.assign_hbm), channel_id=1, source_target_pairs={{0,1},{1,0},{2,3},{3,2},{4,5},{5,4},{6,7},{7,6},{8,9},{9,8},{10,11... | collective-permute-start | bytes 18440 | tf_op jit(solution)/shard_map/ppermute | solution.py:357
  13.4 0.6 copy-start.3
  25.2 2.6 %copy-start = (f32[168,3072]{1,0:T(8,128)S(1)}, f32[168,3072]{1,0:T(8,128)}, u32[]{:S(2)}) copy-start(f32[168,3072]{1,0:T(8,128)} %get-tuple-element.8.early_ref) | copy-start | bytes 6193156
  25.2 2.6 %copy-start.1 = (bf16[384,768]{1,0:T(8,128)(2,1)S(1)}, bf16[384,768]{1,0:T(8,128)(2,1)}, u32[]{:S(2)}) copy-start(bf16[384,768]{1,0:T(8,128)(2,1)} %get-tuple-element.9.turned_ref) | copy-start | bytes 1769476
  25.8 1.9 %collective-permute-start.3 = (f32[128,896]{1,0:T(8,128)S(1)}, f32[128,896]{1,0:T(8,128)S(1)}, u32[]{:S(2)}, u32[]{:S(2)}) collective-permute-start(f32[128,896]{1,0:T(8,128)S(1)} %shard_map.88), channel_id=1, source_target_pairs={{0,1},{1,0},{2,3},{3,2},{4,5},{5,4},{6,7},{7,6},{8,9},{9,8},{10,11... | collective-permute-start | bytes 1376264 | tf_op jit(solution)/shard_map/ppermute | solution.py:391
  60.7 1.4 %collective-permute-start.4 = (bf16[384,256]{1,0:T(8,128)(2,1)S(1)}, bf16[384,256]{1,0:T(8,128)(2,1)S(1)}, u32[]{:S(2)}, u32[]{:S(2)}) collective-permute-start(bf16[384,256]{1,0:T(8,128)(2,1)S(1)} %bitcast.12), channel_id=1, source_target_pairs={{0,1},{1,0},{2,3},{3,2},{4,5},{5,4},{6,7},{7,6},{8,9},{9,8},{10,11... | collective-permute-start | bytes 589832 | tf_op jit(solution)/shard_map/ppermute | solution.py:420

commit v5 on v4

--- a/solution.py
+++ b/solution.py
@@ -119,7 +119,7 @@
 def rotate_kernel(
     points_hbm, points_other_hbm, codes_hbm, codes_other_hbm, assign_hbm, assign_other_hbm, rotation_hbm,
     out_hbm, early_hbm, turned_hbm,
-    points_ref, codes_ref, assign_ref, rotation_ref, out_ref, turned_ref, note_ref, in_sems, out_sems,
+    points_ref, codes_ref, assign_ref, assign_other_ref, rotation_ref, out_ref, turned_ref, note_ref, in_sems, out_sems,
 ):
     width, count = out_ref.shape
     own = count // 2
@@ -140,8 +140,8 @@
         (
             (codes_hbm, codes_ref.at[0]),
             (codes_other_hbm, codes_ref.at[1]),
-            (assign_hbm, assign_ref.at[0]),
-            (assign_other_hbm, assign_ref.at[1]),
+            (assign_hbm, assign_ref),
+            (assign_other_hbm, assign_other_ref),
         )
     ):
         notes.append(pltpu.make_async_copy(source, target, in_sems.at[1 + 2 * PIECES + k]))
@@ -175,7 +175,9 @@
         for start in range(0, subspaces, SIDE):
             note_ref[2 * start : 2 * start + SIDE, part] = low[start : start + SIDE]
             note_ref[2 * start + SIDE : 2 * (start + SIDE), part] = high[start : start + SIDE]
-        note_ref[2 * subspaces :, part] = jnp.broadcast_to(assign_ref[side].astype(jnp.float32), (8, own))
+        note_ref[2 * subspaces :, part] = jnp.broadcast_to(
+            (assign_ref, assign_other_ref)[side][...].reshape(1, own).astype(jnp.float32), (8, own)
+        )
     lines, after = 2 * SHARES[0] * SIDE, 2 * subspaces
     for k, (source, target) in enumerate(
         (
@@ -251,7 +253,6 @@
     first_half = lax.broadcasted_iota(jnp.int32, (tile, count), 0) < HIGH
     spot = lax.broadcasted_iota(jnp.int32, (8, LANES), 1) // LOW
     line = lax.broadcasted_iota(jnp.int32, (8, LANES), 0)
-    wide_line = lax.broadcasted_iota(jnp.int32, (8, CODEWORDS), 0)
     one, zero = jnp.ones((), jnp.bfloat16), jnp.zeros((), jnp.bfloat16)
     spots = LANES // LOW
 
@@ -303,11 +304,11 @@
         for base in range(starts[share], ends[share], SIDE):
             pending += spread(base)
             while len(pending) >= GROUP:
-                lines = [jnp.concatenate(halves, axis=1) for halves, _ in pending[:GROUP]]
-                tally = jnp.zeros((8, CODEWORDS), jnp.float32)
-                for place, (_, tallies) in enumerate(pending[:GROUP]):
-                    row = jnp.broadcast_to(jnp.concatenate(tallies, axis=1), (8, CODEWORDS))
-                    tally = jnp.where(wide_line == place, row, tally)
+                lines = [halves[side] for side in range(2) for halves, _ in pending[:GROUP]]
+                tally = jnp.zeros((8, LANES), jnp.float32)
+                for place in range(2 * GROUP):
+                    row = pending[place % GROUP][1][place // GROUP]
+                    tally = jnp.where(line == place, jnp.broadcast_to(row, (8, LANES)), tally)
                 out_ref[done] = jnp.concatenate(lines + [tally], axis=0).astype(jnp.bfloat16)
                 pending, done = pending[GROUP:], done + 1
     store.wait()
@@ -351,7 +352,7 @@
     )(child_centroids, child_sizes[None, :], parent_of[None, :])
     near = lax.all_to_all(packed.reshape(chips, most, width), ("lists", "z"), 0, 0)
     half_width, half_subspaces, pair_count = width // 2, subspaces // 2, 2 * count
-    turned_codes, parent_row = codes.T, assign[None, :]
+    turned_codes, parent_row = codes.T, assign
 
     def both(array):
         return array, lax.ppermute(array, "core", SWAP)
@@ -370,7 +371,8 @@
         scratch_shapes=[
             pltpu.VMEM((pair_count, width), jnp.bfloat16),
             pltpu.VMEM((2, subspaces, count), jnp.int32),
-            pltpu.VMEM((2, 1, count), jnp.int32),
+            pltpu.VMEM((count,), jnp.int32),
+            pltpu.VMEM((count,), jnp.int32),
             pltpu.VMEM((width, width), jnp.bfloat16),
             pltpu.VMEM((half_width, pair_count), jnp.float32),
             pltpu.VMEM((half_width, width), jnp.bfloat16),
@@ -390,10 +392,11 @@
     )(near.reshape(chips * most, width), rotated)
     sums_of_list = mine + lax.ppermute(mine, "core", SWAP)
     groups = half_subspaces // GROUP
-    rows = GROUP * (width // subspaces) + 8
+    tops = GROUP * (width // subspaces)
+    rows = 2 * tops + 8
     sums, merged = pl.pallas_call(
         code_kernel,
-        out_shape=(shaped((groups, rows, CODEWORDS), jnp.bfloat16), shaped((shard_rows, width))),
+        out_shape=(shaped((groups, rows, LANES), jnp.bfloat16), shaped((shard_rows, width))),
         in_specs=whole(3) + anywhere(1),
         out_specs=tuple(whole(1) + anywhere(1)),
         scratch_shapes=[
@@ -407,16 +410,18 @@
     )(sums_of_list, early, turned, rotated)
 
     splits = chips // groups
-    chip = sums.reshape(groups, rows, splits, CODEWORDS // splits)
-    chip = chip.transpose(0, 2, 1, 3).reshape(chips, rows, CODEWORDS // splits)
+    part = LANES // splits
+    chip = sums.reshape(groups, rows, splits, part).transpose(0, 2, 1, 3).reshape(chips, rows, part)
     total = jnp.sum(lax.all_to_all(chip, ("lists", "z"), 0, 0).astype(jnp.float32), axis=0)
-    sub_width = (rows - 8) // GROUP
-    tops = total[: rows - 8].reshape(GROUP, sub_width, -1)
-    means = tops / (1.0 + total[rows - 8 : rows - 8 + GROUP, None, :])
-    means = means.reshape(1, rows - 8, -1).astype(jnp.bfloat16)
-    means = jnp.broadcast_to(means, (chips,) + means.shape[1:])
+    counts = total[2 * tops : 2 * tops + 2 * GROUP].reshape(2, GROUP, 1, part)
+    means = total[: 2 * tops].reshape(2, GROUP, tops // GROUP, part) / (1.0 + counts)
+    means = means.reshape(2, tops, part).astype(jnp.bfloat16)
+    means = jnp.concatenate([means[0], means[1]], axis=1)
+    means = jnp.broadcast_to(means[None], (chips, tops, 2 * part))
     mine = lax.all_to_all(means, ("lists", "z"), 0, 0)
-    mine = mine.reshape(groups, splits, rows - 8, -1).transpose(0, 2, 1, 3).reshape(-1, CODEWORDS)
+    if splits > 1:
+        mine = mine.reshape(groups, splits, tops, 2, part).transpose(0, 2, 3, 1, 4)
+    mine = mine.reshape(groups * tops, CODEWORDS)
     other = lax.ppermute(mine, "core", SWAP)
     first = core == 0
     means = jnp.concatenate([jnp.where(first, mine, other), jnp.where(first, other, mine)], axis=0)

time: 63.5 us -> 62.7 us (0.987)
  blocking collectives: 25.4 us -> 24.6 us
  local copies, waits for them, and re-layouts: 1.31 us -> 0.63 us
    all_to_all x1, blocking collectives: 13.8 us -> 13 us  [body(): lax.all_to_all(chip, ('lists', 'z'), 0, 0).astype(jnp.float32)]
    broadcast_in_dim x2 -> x1, local copies, waits for them, and re-layouts: 0.72 us -> 0.01 us  [body(): means = jnp.broadcast_to(means[None], (chips, tops, 2 * part))]
  transfers between devices with their start and end apart: 6 -> 6, of which waited for: 4 -> 4; matrix products, arithmetic and copies ran while one was open for 1% -> 0% of each run, Pallas kernels for 13% -> 13%
where the time goes in v5:
time: 62.7 us; the launch traced here: 62.4 us
  blocking collectives  24.6 us (39%)
  Pallas kernels  16.4 us (26%)
  waiting for transfers between devices  9.96 us (16%)
  starting transfers between devices  9.05 us (14%)
  other arithmetic  1.09 us (2%)
  between operations  0.76 us (1%)
  local copies, waits for them, and re-layouts  0.63 us (1%)
    all_to_all x1, blocking collectives, body(): lax.all_to_all(chip, ('lists', 'z'), 0, 0).astype(jnp.float32)  13 us
    all_to_all x1, blocking collectives, body(): mine = lax.all_to_all(means, ('lists', 'z'), 0, 0)  11.5 us
    all_to_all x1, starting transfers between devices, body(): lax.all_to_all(packed.reshape(chips, most, width), ('lists', 'z'), 0, 0)  8.3 us
    pallas_call x1, Pallas kernels, body(): pl.pallas_call(code_kernel, out_shape=(shaped((groups, rows, LANES), jnp....  7.49 us
    pallas_call x1, Pallas kernels, body(): pl.pallas_call(rotate_kernel, out_shape=(shaped((SLABS, half_width, pair_...  6.23 us
    all_to_all x1, waiting for transfers between devices, body(): lax.all_to_all(packed.reshape(chips, most, width), ('lists', 'z'), 0, 0)  5.34 us
    pallas_call x1, Pallas kernels, body(): pl.pallas_call(functools.partial(pack_kernel, owner_parents), out_shape=s...  1.99 us
    ppermute x1, waiting for transfers between devices, body(): sums_of_list = mine + lax.ppermute(mine, 'core', SWAP)  1.8 us
  transfers between devices with their start and end apart: 6, of which 4 were waited for; matrix products, arithmetic and copies ran while one was open for 0% of the time, Pallas kernels for 13%

profile of v5, /device:TPU:0, one launch (start us, length us, event | category | flops | bytes accessed | tf_op | source)
XLA Modules:
  0.0 62.4 jit_solution(18037084179621917581)
XLA Ops:
  0.6 0.5 collective-permute-start
  1.1 0.1 collective-permute-start.1
  1.2 2.0 %shard_map.86 = s16[4,4,16,768]{3,2,1,0:T(8,128)(2,1)} custom-call(f32[32,768]{1,0:T(8,128)} %child_hbm.1, s32[1,32]{1,0:T(1,128)} %bitcast.23, s32[1,32]{1,0:T(1,128)} %bitcast.24), custom_call_target="tpu_custom_call" | custom-call | tf_op jit(solution)/shard_map/pallas_call | solution.py:340
  3.2 8.3 %all-to-all-start = ((s16[16,16,768]{2,1,0:T(8,128)(2,1)}), s16[16,16,768]{2,1,0:T(8,128)(2,1)S(1)}, u32[]{:S(2)}, u32[]{:S(2)}) async-start(s16[16,16,768]{2,1,0:T(8,128)(2,1)} %bitcast.18), calls=%async_computation | async-start | bytes 786432 | tf_op jit(solution)/shard_map/all_to_all | solution.py:353
  11.5 0.1 collective-permute-start.2
  11.6 1.4 %collective-permute-done.2.assign_other_hbm = s32[1536]{0:T(1024)S(1)} collective-permute-done((s32[1536]{0:T(1024)}, s32[1536]{0:T(1024)S(1)}, u32[]{:S(2)}, u32[]{:S(2)}) %collective-permute-start.2) | collective-permute-done | bytes 6176 | tf_op jit(solution)/shard_map/ppermute | solution.py:358
  13.0 0.0 copy-start.2
  13.0 0.0 collective-permute-done.1.codes_other_hbm
  13.0 0.0 collective-permute-done.points_other_hbm
  13.0 0.6 copy-done.2
  13.6 6.2 %shard_map.87 = (f32[4,384,3072]{2,1,0:T(8,128)}, f32[168,3072]{1,0:T(8,128)}, bf16[384,768]{1,0:T(8,128)(2,1)}) custom-call(bf16[1536,768]{1,0:T(8,128)(2,1)} %points_hbm.1, bf16[1536,768]{1,0:T(8,128)(2,1)} %collective-permute-done.points_other_hbm, s32[96,1536]{1,0:T(8,128)} %bitcast.21, s32[96,1536]{1,0:T(8,128)} %collective-permute-done.1.codes_other_hbm, ...), custom_call_target="tpu_custom_call" | custom-call | flops 1811939328 | bytes 14680064 | tf_op jit(solution)/shard_map/pallas_call | solution.py:362
  19.8 5.3 %all-to-all-done = s16[16,16,768]{2,1,0:T(8,128)(2,1)S(1)} async-done(((s16[16,16,768]{2,1,0:T(8,128)(2,1)}), s16[16,16,768]{2,1,0:T(8,128)(2,1)S(1)}, u32[]{:S(2)}, u32[]{:S(2)}) %all-to-all-start) | async-done | bytes 393248 | tf_op jit(solution)/shard_map/all_to_all | solution.py:353
  25.2 0.0 copy-start
  25.2 0.0 copy-start.1
  25.2 0.7 %shard_map.88 = f32[128,896]{1,0:T(8,128)S(1)} custom-call(s16[256,768]{1,0:T(8,128)(2,1)S(1)} %bitcast.17, f32[4,384,3072]{2,1,0:T(8,128)} %get-tuple-element.7.after_ref.rotated_hbm), custom_call_target="tpu_custom_call" | custom-call | tf_op jit(solution)/shard_map/pallas_call | solution.py:386
  25.8 0.1 collective-permute-start.3
  25.9 1.8 %collective-permute-done.3 = f32[128,896]{1,0:T(8,128)S(1)} collective-permute-done((f32[128,896]{1,0:T(8,128)S(1)}, f32[128,896]{1,0:T(8,128)S(1)}, u32[]{:S(2)}, u32[]{:S(2)}) %collective-permute-start.3) | collective-permute-done | bytes 458784 | tf_op jit(solution)/shard_map/ppermute | solution.py:393
  27.7 0.1 add.17.whole_ref
  27.8 0.0 copy-done
  27.8 0.0 copy-done.1
  27.8 7.5 %shard_map.89 = (bf16[16,56,128]{2,1,0:T(8,128)(2,1)S(1)}, f32[16,768]{1,0:T(8,128)}) custom-call(f32[128,896]{1,0:T(8,128)S(1)} %add.17.whole_ref, f32[168,3072]{1,0:T(8,128)S(1)} %copy-done, bf16[384,768]{1,0:T(8,128)(2,1)S(1)} %copy-done.1, f32[4,384,3072]{2,1,0:T(8,128)} %get-tuple-element.7.after_ref.rotated_hbm), custom_call_target="tpu_custom_call" | custom-call | tf_op jit(solution)/shard_map/pallas_call | solution.py:397
  35.3 13.0 %all_to_all.15 = bf16[16,56,128]{2,1,0:T(8,128)(2,1)S(1)} all-to-all(bf16[16,56,128]{2,1,0:T(8,128)(2,1)S(1)} %get-tuple-element.11), channel_id=1, replica_groups=mesh['lists'=4,'z'=4,'core'=2] {'lists','z'}, dimensions={0} | all-to-all | bytes 458752 | tf_op jit(solution)/shard_map/all_to_all | solution.py:415
  48.5 11.5 %all_to_all.16 = bf16[16,24,256]{2,1,0:T(8,128)(2,1)S(1)} all-to-all(bf16[16,24,256]{2,1,0:T(8,128)(2,1)S(1)} %broadcast_in_dim.14), channel_id=1, replica_groups=mesh['lists'=4,'z'=4,'core'=2] {'lists','z'}, dimensions={0} | all-to-all | bytes 393216 | tf_op jit(solution)/shard_map/all_to_all | solution.py:421
  60.0 0.0 collective-permute-start.4
  60.0 1.4 %collective-permute-done.4 = bf16[384,256]{1,0:T(8,128)(2,1)S(1)} collective-permute-done((bf16[384,256]{1,0:T(8,128)(2,1)S(1)}, bf16[384,256]{1,0:T(8,128)(2,1)S(1)}, u32[]{:S(2)}, u32[]{:S(2)}) %collective-permute-start.4) | collective-permute-done | bytes 196640 | tf_op jit(solution)/shard_map/ppermute | solution.py:425
  61.5 0.9 %maximum_convert_fusion = f32[768,256]{1,0:T(8,128)} fusion(bf16[384,256]{1,0:T(8,128)(2,1)S(1)} %get-tuple-element.13, bf16[384,256]{1,0:T(8,128)(2,1)S(1)} %get-tuple-element.12), kind=kLoop, calls=%fused_computation.1 | loop fusion | flops 786432 | bytes 1179648 | tf_op jit(solution)/shard_map/convert_element_type | solution.py:428
  (9 shorter events, 0.1 us)
Async XLA Ops:
  0.6 12.4 %collective-permute-start = (bf16[1536,768]{1,0:T(8,128)(2,1)}, bf16[1536,768]{1,0:T(8,128)(2,1)}, u32[]{:S(2)}, u32[]{:S(2)}) collective-permute-start(bf16[1536,768]{1,0:T(8,128)(2,1)} %points_hbm.1), channel_id=1, source_target_pairs={{0,1},{1,0},{2,3},{3,2},{4,5},{5,4},{6,7},{7,6},{8,9},{9,8},{10,11... | collective-permute-start | bytes 7077896 | tf_op jit(solution)/shard_map/ppermute | solution.py:358
  1.1 11.8 %collective-permute-start.1 = (s32[96,1536]{1,0:T(8,128)}, s32[96,1536]{1,0:T(8,128)}, u32[]{:S(2)}, u32[]{:S(2)}) collective-permute-start(s32[96,1536]{1,0:T(8,128)} %bitcast.20), channel_id=1, source_target_pairs={{0,1},{1,0},{2,3},{3,2},{4,5},{5,4},{6,7},{7,6},{8,9},{9,8},{10,11... | collective-permute-start | bytes 1769480 | tf_op jit(solution)/shard_map/ppermute | solution.py:358
  3.2 21.9 %all-to-all-start = ((s16[16,16,768]{2,1,0:T(8,128)(2,1)}), s16[16,16,768]{2,1,0:T(8,128)(2,1)S(1)}, u32[]{:S(2)}, u32[]{:S(2)}) async-start(s16[16,16,768]{2,1,0:T(8,128)(2,1)} %bitcast.18), calls=%async_computation | async-start | bytes 786432 | tf_op jit(solution)/shard_map/all_to_all | solution.py:353
  11.5 1.4 %collective-permute-start.2 = (s32[1536]{0:T(1024)}, s32[1536]{0:T(1024)S(1)}, u32[]{:S(2)}, u32[]{:S(2)}) collective-permute-start(s32[1536]{0:T(1024)} %assign_hbm.1), channel_id=1, source_target_pairs={{0,1},{1,0},{2,3},{3,2},{4,5},{5,4},{6,7},{7,6},{8,9},{9,8},{10,11... | collective-permute-start | bytes 18440 | tf_op jit(solution)/shard_map/ppermute | solution.py:358
  13.0 0.6 copy-start.2
  25.2 2.6 %copy-start = (f32[168,3072]{1,0:T(8,128)S(1)}, f32[168,3072]{1,0:T(8,128)}, u32[]{:S(2)}) copy-start(f32[168,3072]{1,0:T(8,128)} %get-tuple-element.8.early_ref) | copy-start | bytes 6193156
  25.2 2.6 %copy-start.1 = (bf16[384,768]{1,0:T(8,128)(2,1)S(1)}, bf16[384,768]{1,0:T(8,128)(2,1)}, u32[]{:S(2)}) copy-start(bf16[384,768]{1,0:T(8,128)(2,1)} %get-tuple-element.9.turned_ref) | copy-start | bytes 1769476
  25.8 1.9 %collective-permute-start.3 = (f32[128,896]{1,0:T(8,128)S(1)}, f32[128,896]{1,0:T(8,128)S(1)}, u32[]{:S(2)}, u32[]{:S(2)}) collective-permute-start(f32[128,896]{1,0:T(8,128)S(1)} %shard_map.88), channel_id=1, source_target_pairs={{0,1},{1,0},{2,3},{3,2},{4,5},{5,4},{6,7},{7,6},{8,9},{9,8},{10,11... | collective-permute-start | bytes 1376264 | tf_op jit(solution)/shard_map/ppermute | solution.py:393
  60.0 1.4 %collective-permute-start.4 = (bf16[384,256]{1,0:T(8,128)(2,1)S(1)}, bf16[384,256]{1,0:T(8,128)(2,1)S(1)}, u32[]{:S(2)}, u32[]{:S(2)}) collective-permute-start(bf16[384,256]{1,0:T(8,128)(2,1)S(1)} %bitcast.19), channel_id=1, source_target_pairs={{0,1},{1,0},{2,3},{3,2},{4,5},{5,4},{6,7},{7,6},{8,9},{9,8},{10,11... | collective-permute-start | bytes 589832 | tf_op jit(solution)/shard_map/ppermute | solution.py:425
